TPU v7x, 128 devices: a whole 4x4x4 slice. The times are simulated.
128 devices in a mesh: tgt: 16 (over y, x), src: 8 (over z, core).
Axes of the slice: x: 4, y: 4, z: 4, core: 2. Of those that a mesh axis runs over, the one named last changes fastest.
Arguments:
- charges: bfloat16 [8, 131072], P(None, 'src'), may hold values from -6 to 6
- weights: float32 [131072], P('tgt'), may hold values from 0.4 to 7.5
- cell_order: int32 [128, 1024], P(('tgt', 'src')), may hold values from 0 to 1023, as said below
- leaf_coords: int32 [3, 128], replicated, may hold values from 0 to 7, as said below
- near_src: int32 [128, 27], P('tgt'), may hold values from -1 to 127, as said below
Outputs:
- potential: bfloat16 [8, 131072], P(None, ('tgt', 'src'))
- root_factor: float32 [64, 64], replicated
Inputs may be any that keep to these rules, and one draw needn't show every extreme that they name: `cell_order`: each row is a permutation of 0 to 1023. `leaf_coords`: distinct positions on a grid of 8 x 4 x 4 leaf boxes. `near_src`: row l lists in increasing order every leaf whose coordinates differ from leaf l's by at most one in each dimension, l itself included, then -1.
All inputs are finite; a program needn't handle non-finite values.
Results may differ from a plain program's by a relative error of at most 0.0013.
The roundings to bfloat16 on the way count: a program that leaves them out, or rounds other values in their place, can miss the bound.
Values may be sent and summed in bfloat16 or wider, within the bound.
A program may use at most 64 MiB of HBM per device.

v0:
```python
import math

import jax
import jax.numpy as jnp
from jax import lax
from jax.sharding import PartitionSpec as P

EDGE = 8


def combined_all(value, axis, join):
    pieces = lax.all_gather(value, axis)
    head = pieces[0]
    tail = pieces[1:]
    so_far, _ = lax.scan(lambda so_far, share: (join(so_far, share), None), head, tail)
    return so_far


def chebyshev_nodes(extent):
    number = jnp.arange(4, dtype=jnp.float32)
    return extent * 0.5 + extent * 0.5 * jnp.cos((2.0 * number + 1.0) * (math.pi / 8.0))


def lagrange(points, node_list):
    columns = []
    for node_a in range(4):
        factor = jnp.ones_like(points)
        for node_b in range(4):
            if node_b != node_a:
                factor = (
                    factor * (points - node_list[node_b]) / (node_list[node_a] - node_list[node_b])
                )
        columns.append(factor)
    return jnp.stack(columns, axis=1)


def in_leaf(order_row, edge_cells):
    plane = 2 * edge_cells * edge_cells
    along_x = order_row // plane
    along_y = order_row // (2 * edge_cells) % edge_cells
    along_z = order_row % (2 * edge_cells)
    return jnp.stack([along_x, along_y, along_z]).astype(jnp.float32) + 0.5


def leaf_basis(edge_cells):
    cell_ids = jnp.arange(2 * edge_cells**3, dtype=jnp.int32)
    placed = in_leaf(cell_ids, edge_cells)
    along_x = lagrange(placed[0], chebyshev_nodes(1.0 * edge_cells))
    along_y = lagrange(placed[1], chebyshev_nodes(1.0 * edge_cells))
    along_z = lagrange(placed[2], chebyshev_nodes(2.0 * edge_cells))
    joined = along_x[:, :, None, None] * along_y[:, None, :, None] * along_z[:, None, None, :]
    return joined.reshape(cell_ids.shape[0], 64)


def node_offsets(edge_cells):
    node_x = chebyshev_nodes(1.0 * edge_cells)
    node_z = chebyshev_nodes(2.0 * edge_cells)
    first = jnp.broadcast_to(node_x[:, None, None], (4, 4, 4)).reshape(64)
    second = jnp.broadcast_to(node_x[None, :, None], (4, 4, 4)).reshape(64)
    third = jnp.broadcast_to(node_z[None, None, :], (4, 4, 4)).reshape(64)
    return jnp.stack([first, second, third], axis=1)


def cell_positions(order_row, leaf_coord, spacing, edge_cells):
    return leaf_coord[:, None] * spacing[:, None] + in_leaf(order_row, edge_cells)


def kernel(tgt_points, src_points):
    between = tgt_points[:, :, None] - src_points[:, None, :]
    distance = jnp.sum(between * between, axis=0)
    return 0.05 / jnp.sqrt(distance + 1.0)


def join_factors(upper_one, upper_two):
    highest = lax.Precision.HIGHEST
    stacked = jnp.dot(upper_one.T, upper_one, precision=highest) + jnp.dot(
        upper_two.T, upper_two, precision=highest
    )
    return jnp.linalg.cholesky(stacked).T


def near_sum(
    picked,
    near_flat,
    slot_width,
    first_target,
    row_count,
    orders,
    coords_f,
    spacing,
    source_data,
    scenarios,
    leaf_size,
):
    slot_total = near_flat.shape[0]
    position = jnp.cumsum(picked.astype(jnp.int32)) - 1
    live_count = jnp.sum(picked.astype(jnp.int32))
    worklist = (
        jnp.zeros((slot_total,), jnp.int32)
        .at[jnp.where(picked, position, slot_total)]
        .set(jnp.arange(slot_total, dtype=jnp.int32), mode="drop")
    )

    def near_step(number, summed):
        slot_index = worklist[number]
        local_target = slot_index // slot_width
        target = first_target + local_target
        source = near_flat[slot_index]
        tgt_points = cell_positions(orders[target], coords_f[:, target], spacing, EDGE)
        src_points = cell_positions(orders[source], coords_f[:, source], spacing, EDGE)
        kernel_block = kernel(tgt_points, src_points).astype(jnp.bfloat16)
        source_charges = lax.dynamic_slice_in_dim(source_data, source * leaf_size, leaf_size, 1)
        contrib = lax.dot_general(
            source_charges,
            kernel_block,
            (((1,), (1,)), ((), ())),
            preferred_element_type=jnp.float32,
        )
        previous = lax.dynamic_slice_in_dim(summed, local_target * leaf_size, leaf_size, 1)
        return lax.dynamic_update_slice_in_dim(
            summed, previous + contrib, local_target * leaf_size, 1
        )

    return lax.fori_loop(
        0, live_count, near_step, jnp.zeros((scenarios, row_count * leaf_size), jnp.float32)
    )


def shards(charges, weights, cell_order, leaf_coords, near_src):
    highest = lax.Precision.HIGHEST
    src_count = lax.axis_size("src")
    tgt_index = lax.axis_index("tgt")
    src_index = lax.axis_index("src")
    orders = lax.all_gather(cell_order, ("tgt", "src"), axis=0, tiled=True)
    leaves = orders.shape[0]
    leaf_size = orders.shape[1]
    tgt_leaves = near_src.shape[0]
    slot_width = near_src.shape[1]
    scenarios = charges.shape[0]
    src_leaves = charges.shape[1] // leaf_size
    spacing = jnp.array([EDGE, EDGE, 2 * EDGE], dtype=jnp.float32)
    coords_f = leaf_coords.astype(jnp.float32)
    tgt_start = tgt_index * tgt_leaves
    src_start = src_index * src_leaves
    lagrange_basis = leaf_basis(EDGE)
    leaf_nodes = coords_f.T[:, None, :] * spacing[None, None, :] + node_offsets(EDGE)[None]
    tgt_orders = lax.dynamic_slice_in_dim(orders, tgt_start, tgt_leaves, 0)
    tgt_bases = lagrange_basis[tgt_orders]
    near_flat = near_src.reshape(-1)
    live = near_flat >= 0
    live_rank = jnp.cumsum(live.astype(jnp.int32)) - 1
    picked = live & (live_rank % src_count == src_index)
    gathered = lax.all_gather(charges, "src", axis=1, tiled=True)
    near_part = near_sum(
        picked,
        near_flat,
        slot_width,
        tgt_start,
        tgt_leaves,
        orders,
        coords_f,
        spacing,
        gathered,
        scenarios,
        leaf_size,
    )
    src_orders = lax.dynamic_slice_in_dim(orders, src_start, src_leaves, 0)
    src_bases = lagrange_basis[src_orders]
    local_charges = charges.astype(jnp.float32).reshape(scenarios, src_leaves, leaf_size)
    moments = jnp.einsum("lje,slj->les", src_bases, local_charges, precision=highest)
    tgt_nodes = lax.dynamic_slice_in_dim(leaf_nodes, tgt_start, tgt_leaves, 0)
    src_nodes = lax.dynamic_slice_in_dim(leaf_nodes, src_start, src_leaves, 0)
    src_ids = src_start + jnp.arange(src_leaves, dtype=jnp.int32)
    near_mask = jnp.any(near_src[:, :, None] == src_ids[None, None, :], axis=1)

    def couple(target):
        between = tgt_nodes[target][:, None, None, :] - src_nodes[None, :, :, :]
        distance = jnp.sum(between * between, axis=3)
        keep = 1.0 - near_mask[target].astype(jnp.float32)
        coupling = 0.05 / jnp.sqrt(distance + 1.0) * keep[None, :, None]
        return jnp.einsum("ebf,bfs->es", coupling, moments, precision=highest)

    local_sums = lax.map(couple, jnp.arange(tgt_leaves, dtype=jnp.int32))
    far_part = jnp.einsum("lje,les->slj", tgt_bases, local_sums, precision=highest).reshape(
        scenarios, tgt_leaves * leaf_size
    )
    partial_sums = weights[None, :] * (near_part + far_part)
    potential = lax.psum_scatter(partial_sums, "src", scatter_dimension=1, tiled=True).astype(
        jnp.bfloat16
    )
    weighted = weights.reshape(tgt_leaves, leaf_size)[:, :, None] * tgt_bases
    gram_matrix = jnp.einsum("lje,ljf->ef", weighted, weighted, precision=highest)
    root_factor = combined_all(jnp.linalg.cholesky(gram_matrix).T, "tgt", join_factors)
    root_factor = root_factor / jnp.sqrt(jnp.float32(leaves * leaf_size))
    return (potential, root_factor)


def solution(mesh):
    placed = (P(None, "src"), P("tgt"), P(("tgt", "src"), None), P(), P("tgt", None))
    return jax.shard_map(
        shards,
        mesh=mesh,
        in_specs=placed,
        out_specs=(P(None, ("tgt", "src")), P()),
        check_vma=False,
    )
```

profile of v0, /device:TPU:6, one launch (start us, length us, event | category | flops | bytes accessed | tf_op | source)
XLA Modules:
  0.0 682.0 jit_solution(14837322529147683513)
XLA Ops:
  40.1 37.7 %all-gather.1 = s32[128,1,1024]{2,1,0:T(1,128)S(1)} all-gather(s32[1,1,1024]{2,1,0:T(1,128)} %bitcast.142), channel_id=1, replica_groups=mesh['tgt'=16,'src'=8] {'tgt','src'}, dimensions={0}, use_global_device_ids=true | all-gather | bytes 528384 | tf_op jit(solution)/shard_map/all_gather | solution.py:134
  93.8 54.4 %gather_fusion = f32[16384,64]{1,0:T(8,128)} fusion(f32[1024,64]{1,0:T(8,128)S(1)} %copy.60, s32[16384]{0:T(1024)S(1)} %broadcast_clamp_fusion), kind=kCustom, calls=%fused_computation | custom fusion | bytes 8454144 | tf_op jit(solution)/shard_map/gather | solution.py:168
  153.4 31.6 %while.34 = (s32[]{:T(128)}, f32[8,64,8]{1,2,0:T(8,128)S(1)}, s32[8]{0:T(128)S(1)}, f32[8,64,3]{1,0,2:T(8,128)S(1)}, f32[16,64,3]{1,0,2:T(8,128)S(1)}, /*index=5...) while((s32[]{:T(128)}, f32[8,64,8]{1,2,0:T(8,128)S(1)}, ...), condition=%wide.region_12.13_spmd, body=%wide.region_10.12_spmd.sunk | while | flops 6946869 | bytes 1398327 | solution.py:183
  185.3 27.7 %gather_fusion.1 = f32[8192,64]{1,0:T(8,128)} fusion(f32[1024,64]{1,0:T(8,128)S(1)} %copy.60, s32[8192]{0:T(1024)S(1)} %bitcast_clamp_fusion), kind=kCustom, calls=%fused_computation.1 | custom fusion | bytes 4227072 | tf_op jit(solution)/shard_map/gather | solution.py:148
  217.7 5.8 cholesky.55
  225.0 22.0 %all-gather = f32[1024,64]{1,0:T(8,128)S(1)} all-gather(f32[64,64]{1,0:T(8,128)S(1)} %copy.67), channel_id=2, replica_groups=mesh['tgt'=16,'src'=8] {'tgt'}, dimensions={0}, use_global_device_ids=true | all-gather | bytes 278528 | tf_op jit(solution)/shard_map/all_gather | solution.py:12
  250.6 5.2 fusion.49
  255.8 300.4 %while.36 = (s32[]{:T(128)}, f32[8,8192]{1,0:T(8,128)S(1)}, s32[]{:T(128)}, s32[216]{0:T(256)S(1)}, s32[216]{0:T(256)S(1)}, /*index=5*/bf16[8,131072]{1,0:T(8,12...) while((s32[]{:T(128)}, f32[8,8192]{1,0:T(8,128)S(1)}, ...), condition=%wide.region_8.9_spmd.clone, body=%wide.region_6.8_spmd.sunk.clone.sunk | while | flops 28434468 | bytes 8594039 | solution.py:124
  557.0 116.1 %while.35 = (s32[]{:T(128)}, f32[64,64]{0,1:T(8,128)S(1)}, f32[15,64,64]{2,1,0:T(8,128)S(1)}, s32[]{:T(128)}) while((s32[]{:T(128)}, f32[64,64]{0,1:T(8,128)S(1)}, f32[15,64,64]{2,1,0:T(8,128)S(1)}, s32[]{:T(128)}) %tuple.114), condition=%wide.region_17.19_spmd, body=%wide.region_16.18_spmd.sunk | while | flops 6328385 | bytes 246339 | solution.py:15
  557.6 5.8 cholesky.117
  565.3 5.8 cholesky.117
  573.0 5.8 cholesky.117
  580.8 5.8 cholesky.117
  588.5 5.8 cholesky.117
  596.2 5.8 cholesky.117
  604.0 5.8 cholesky.117
  611.7 5.8 cholesky.117
  619.5 5.8 cholesky.117
  627.2 5.8 cholesky.117
  634.9 5.8 cholesky.117
  642.7 5.8 cholesky.117
  650.4 5.8 cholesky.117
  658.2 5.8 cholesky.117
  665.9 5.8 cholesky.117
  (455 shorter events, 235.9 us)
Async XLA Ops:
  7.2 248.6 %all-gather.4.cloned.1.call-start = ((), (), s32[]{:S(2)}) async-start(), calls=%async_computation.1 | async-start | bytes 2359296 | tf_op jit(solution)/shard_map/all_gather | solution.py:153
  7.9 665.9 %reduce-scatter.2.cloned.1.call-start = ((), (), s32[]{:S(2)}) async-start(), calls=%async_computation.2 | async-start | bytes 294912 | tf_op jit(solution)/shard_map/reduce_scatter | solution.py:188
  93.8 54.4 %copy-start = (bf16[8,16384]{1,0:T(8,128)(2,1)S(1)}, bf16[8,16384]{1,0:T(8,128)(2,1)}, u32[]{:S(2)}) copy-start(bf16[8,16384]{1,0:T(8,128)(2,1)} %param.13) | copy-start | bytes 786436
  153.4 31.7 %copy-start.2 = (s32[8,27]{1,0:T(8,128)S(1)}, s32[8,27]{1,0:T(8,128)}, u32[]{:S(2)}) copy-start(s32[8,27]{1,0:T(8,128)} %param.17) | copy-start | bytes 2596
  213.0 2.8 copy-start.1
  215.8 40.0 %copy-start.3 = (f32[3,1]{0,1:T(1,128)S(1)}, f32[3,1]{0,1:T(1,128)}, u32[]{:S(2)}) copy-start(f32[3,1]{0,1:T(1,128)} %constant.543) | copy-start | bytes 40
Sparse Core Ops, SparseCore 0:
  9.7 27.7 all-gather.3
  557.1 27.8 reduce-scatter.1
where the time goes:
time: 688 us; the launch traced here: 682 us
  other arithmetic  208 us (30%)
  loops' own time  161 us (23%)
  local copies, waits for them, and re-layouts  124 us (18%)
  matrix products  84 us (12%)
  blocking collectives  59.7 us (9%)
  between operations  44.4 us (6%)
    another operation x1, loops' own time, near_sum(): lax.fori_loop(0, live_count, near_step, jnp.zeros((scenarios, row_count *...  143 us
    another operation x45, other arithmetic, join_factors(): return jnp.linalg.cholesky(stacked).T  97.8 us
    reduce_sum x21, other arithmetic, kernel(): distance = jnp.sum(between * between, axis=0)  66 us
    dot_general x21, matrix products, near_step(): lax.dot_general(source_charges, kernel_block, (((1,), (1,)), ((), ())), p...  60.4 us
    gather x1, local copies, waits for them, and re-layouts, shards(): src_bases = lagrange_basis[src_orders]  54.4 us
    all_gather x1, blocking collectives, shards(): orders = lax.all_gather(cell_order, ('tgt', 'src'), axis=0, tiled=True)  37.7 us
    gather x2, local copies, waits for them, and re-layouts, shards(): tgt_bases = lagrange_basis[tgt_orders]  30.5 us
    all_gather x1, blocking collectives, combined_all(): pieces = lax.all_gather(value, axis)  22 us
  transfers between devices with their start and end apart: 2, of which 0 were waited for; matrix products, arithmetic and copies ran while one was open for 38% of the time, Pallas kernels for 0%

commit v1 on v0

v1 whole, which is shorter than its diff:
```python
import math

import jax
import jax.numpy as jnp
import ml_dtypes
import numpy as np
from jax import lax
from jax.experimental import pallas as pl
from jax.experimental.pallas import tpu as pltpu
from jax.sharding import PartitionSpec as P

EDGE = 8
LEAF = 1024
SCEN = 8
LV = 128
NT = 16
NS = 8
TL = LV // NT
SL = LV // NS
NODES = 64
CELLS = LV * LEAF
MESH = pl.DeviceIdType.MESH
F32 = jnp.float32
BF16 = jnp.bfloat16
NT_DIMS = (((1,), (1,)), ((), ()))


def chebyshev_nodes(extent):
    number = np.arange(4, dtype=np.float64)
    return extent * 0.5 + extent * 0.5 * np.cos((2.0 * number + 1.0) * (math.pi / 8.0))


def lagrange(points, nodes):
    columns = []
    for a in range(4):
        factor = np.ones_like(points)
        for b in range(4):
            if b != a:
                factor = factor * (points - nodes[b]) / (nodes[a] - nodes[b])
        columns.append(factor)
    return np.stack(columns, axis=1)


def basis_table():
    p = np.arange(LEAF)
    along_x = lagrange(p // 128 + 0.5, chebyshev_nodes(8.0))
    along_y = lagrange(p // 16 % 8 + 0.5, chebyshev_nodes(8.0))
    along_z = lagrange(p % 16 + 0.5, chebyshev_nodes(16.0))
    joined = along_x[:, :, None, None] * along_y[:, None, :, None] * along_z[:, None, None, :]
    return joined.reshape(LEAF, NODES).astype(np.float32)


def split_two(table):
    high = table.astype(ml_dtypes.bfloat16)
    low = (table - high.astype(np.float32)).astype(ml_dtypes.bfloat16)
    return high, low


def node_offsets():
    node_x = chebyshev_nodes(8.0)
    node_z = chebyshev_nodes(16.0)
    grid = np.meshgrid(node_x, node_x, node_z, indexing="ij")
    return np.stack([g.reshape(NODES) for g in grid]).astype(np.float32)


def near_table():
    cell = np.arange(128)
    y, z = cell // 16, cell % 16
    delta = np.arange(16)
    blocks = []
    for oy in (-1, 0, 1):
        for oz in (-1, 0, 1):
            dy = y[None, :] - (y[:, None] + 8 * oy)
            dz = z[None, :] - (z[:, None] + 16 * oz)
            square = (dy * dy + dz * dz)[:, None, :] + (delta * delta)[None, :, None]
            value = np.float32(0.05) / np.sqrt(square.astype(np.float32) + np.float32(1.0))
            blocks.append(value.reshape(128, 2048))
    return np.stack(blocks).astype(ml_dtypes.bfloat16)


def exchange_kernel(
    order_ref, w_ref, inv_ref, sq_ref, mine, buf, send_a, recv_a, send_b, recv_b
):
    a = lax.axis_index("tgt")
    b = lax.axis_index("src")
    barrier = pltpu.get_barrier_semaphore()
    home = lax.rem(a, 2) * NS + b
    column = lax.div(a, 2)
    loops_back = b == column

    def signal_sender(k, carry):
        pl.semaphore_signal(
            barrier, 1, device_id=(2 * b + lax.div(k, NS), lax.rem(k, NS)), device_id_type=MESH
        )
        return carry

    def signal_peer(k, carry):
        pl.semaphore_signal(barrier, 1, device_id=(lax.rem(a + k, NT), b), device_id_type=MESH)
        return carry

    own_sender = lax.rem(a, 2) * NS + b
    sends_to_me = lax.div(a, 2) == b

    def signal_other(k, carry):
        at = lax.rem(own_sender + k, NT)
        return signal_sender(at, carry)

    @pl.when(jnp.logical_not(sends_to_me))
    def _():
        signal_other(0, 0)

    lax.fori_loop(1, NT, signal_other, 0)
    lax.fori_loop(1, NT, signal_peer, 0)

    rows = lax.broadcasted_iota(jnp.int32, (8, 128), 0)
    lanes = lax.broadcasted_iota(jnp.int32, (8, 128), 1)
    low_rows = lax.broadcasted_iota(jnp.int32, (128, 128), 0)
    weights = w_ref[pl.ds(pl.multiple_of(b * 8, 8), 8), :]
    square = weights * weights
    placed = jnp.zeros((40, 128), F32)
    for c in range(8):
        order = order_ref[0:1, c * 128 : (c + 1) * 128]
        hit = lax.shift_right_logical(jnp.broadcast_to(order, (8, 128)), 7) == rows
        value = jnp.broadcast_to(square[c : c + 1, :], (8, 128))
        first = value.astype(BF16).astype(F32)
        rest = value - first
        second = rest.astype(BF16).astype(F32)
        third = rest - second
        parts = [jnp.full((8, 128), float(c), F32), lanes.astype(F32), first, second, third]
        left = jnp.concatenate([jnp.where(hit, part, 0.0) for part in parts], axis=0)
        low = jnp.broadcast_to(jnp.bitwise_and(order, 127), (128, 128)) == low_rows
        right = jnp.where(low, 1.0, 0.0).astype(BF16)
        placed = placed + lax.dot_general(
            left.astype(BF16), right, NT_DIMS, preferred_element_type=F32
        )
    inverse = (placed[0:8] * 128.0 + placed[8:16]).astype(jnp.int32)
    mine[...] = inverse
    buf[a] = placed[16:24] + placed[24:32] + placed[32:40]

    pl.semaphore_wait(
        barrier, jnp.where(loops_back, 2 * NT - 2, 2 * NT - 1).astype(jnp.int32)
    )

    def order_copy(k):
        at = lax.rem(a + k, NT)
        return pltpu.make_async_remote_copy(
            src_ref=mine,
            dst_ref=inv_ref.at[home],
            send_sem=send_a.at[k],
            recv_sem=recv_a.at[home],
            device_id=(at, column),
            device_id_type=MESH,
        )

    def square_copy(k):
        return pltpu.make_async_remote_copy(
            src_ref=buf.at[a],
            dst_ref=buf.at[a],
            send_sem=send_b.at[k],
            recv_sem=recv_b.at[a],
            device_id=(lax.rem(a + k, NT), b),
            device_id_type=MESH,
        )

    @pl.when(jnp.logical_not(loops_back))
    def _():
        order_copy(0).start()

    @pl.when(loops_back)
    def _():
        inv_ref[home] = inverse

    def start_both(k, carry):
        order_copy(k).start()
        square_copy(k).start()
        return carry

    lax.fori_loop(1, NT, start_both, 0)

    def order_arrival(slot):
        pltpu.make_async_remote_copy(
            src_ref=mine,
            dst_ref=inv_ref.at[slot],
            send_sem=send_a.at[0],
            recv_sem=recv_a.at[slot],
            device_id=(a, b),
            device_id_type=MESH,
        ).wait_recv()

    def square_arrival(slot):
        pltpu.make_async_remote_copy(
            src_ref=mine,
            dst_ref=buf.at[slot],
            send_sem=send_b.at[0],
            recv_sem=recv_b.at[slot],
            device_id=(a, b),
            device_id_type=MESH,
        ).wait_recv()

    @pl.when(jnp.logical_not(loops_back))
    def _():
        order_arrival(home)
        order_copy(0).wait_send()

    def wait_both(k, carry):
        order_arrival(lax.rem(home + k, NT))
        square_arrival(lax.rem(a + k, NT))
        order_copy(k).wait_send()
        square_copy(k).wait_send()
        return carry

    lax.fori_loop(1, NT, wait_both, 0)
    total = buf[0]
    for k in range(1, NT):
        total = total + buf[k]
    sq_ref[...] = total


def exchange(order, weights):
    return pl.pallas_call(
        exchange_kernel,
        out_shape=(
            jax.ShapeDtypeStruct((SL, 8, 128), jnp.int32),
            jax.ShapeDtypeStruct((8, 128), F32),
        ),
        in_specs=[pl.BlockSpec(memory_space=pltpu.VMEM)] * 2,
        out_specs=(pl.BlockSpec(memory_space=pltpu.VMEM),) * 2,
        scratch_shapes=[
            pltpu.VMEM((8, 128), jnp.int32),
            pltpu.VMEM((NT, 8, 128), F32),
            pltpu.SemaphoreType.DMA((NT,)),
            pltpu.SemaphoreType.DMA((NT,)),
            pltpu.SemaphoreType.DMA((NT,)),
            pltpu.SemaphoreType.DMA((NT,)),
        ],
        compiler_params=pltpu.CompilerParams(collective_id=0, has_side_effects=True),
        name="exchange",
    )(order, weights)


def lane_gather(block, lane):
    return jnp.take_along_axis(block, lane, axis=1, mode="promise_in_bounds")


def permute_row(blocks, index):
    block = lax.shift_right_logical(index, 7)
    lane = jnp.bitwise_and(index, 127)
    out = lane_gather(blocks[0], lane)
    for k in range(1, 8):
        out = jnp.where(block == k, lane_gather(blocks[k], lane), out)
    return out


def local_kernel(
    coords, charges, inv, basis_m, basis_h, basis_l, node_sub, node_lane, table_hbm, out, table, qf, qb, pairs, sem
):
    i = lax.axis_index("tgt")
    j = lax.axis_index("src")
    fetch = pltpu.make_async_copy(table_hbm, table, sem)
    fetch.start()

    def canonical(leaf, carry):
        base = pl.multiple_of(leaf * LEAF, LEAF)
        raw = charges[:, pl.ds(base, LEAF)].astype(F32)
        blocks = [raw[:, k * 128 : (k + 1) * 128] for k in range(8)]
        order = inv[leaf]
        pieces = [
            permute_row(blocks, jnp.broadcast_to(order[x : x + 1, :], (8, 128))) for x in range(8)
        ]
        rows = jnp.concatenate(pieces, axis=0)
        qf[leaf] = rows
        qb[leaf] = rows.astype(BF16)
        return carry

    lax.fori_loop(0, SL, canonical, 0)

    both = jnp.zeros((SL * SCEN, 128), F32)
    for x in range(8):
        rows = qf[:, x * 8 : (x + 1) * 8, :].reshape(SL * SCEN, 128).astype(BF16)
        both = both + jnp.dot(
            rows, basis_m[x * 128 : (x + 1) * 128, :], preferred_element_type=F32
        )
    moments = both[:, :NODES] + both[:, NODES:]

    slot = lax.shift_right_logical(lax.broadcasted_iota(jnp.int32, (1, TL * NODES), 1), 6)
    tgt_box = []
    for d in range(3):
        row = jnp.zeros((1, TL * NODES), jnp.int32)
        for t in range(TL):
            row = jnp.where(slot == t, coords[d, i * TL + t], row)
        tgt_box.append(row)
    spacing = (8.0, 8.0, 16.0)
    tgt_node = [
        tgt_box[d].astype(F32) * spacing[d] + node_lane[d : d + 1, :] for d in range(3)
    ]
    coeff = jnp.zeros((SCEN, TL * NODES), F32)
    for s in range(SL):
        distance = jnp.full((NODES, TL * NODES), 1.0, F32)
        close = jnp.full((1, TL * NODES), True)
        for d in range(3):
            box = coords[d, j * SL + s]
            close = close & (jnp.abs(tgt_box[d] - box) <= 1)
            shifted = tgt_node[d] - box.astype(F32) * spacing[d]
            source = jnp.tile(node_sub[d], (1, TL * NODES // 128))
            between = shifted - source
            distance = distance + between * between
        keep = jnp.where(close, 0.0, 0.05)
        phi = keep / jnp.sqrt(distance)
        high = phi.astype(BF16)
        low = (phi - high.astype(F32)).astype(BF16)
        part = moments[s * 8 : (s + 1) * 8, :]
        part_high = part.astype(BF16)
        part_low = (part - part_high.astype(F32)).astype(BF16)
        twice = jnp.concatenate([part_high.astype(F32), part_low.astype(F32)], axis=0).astype(BF16)
        product = jnp.dot(twice, high, preferred_element_type=F32)
        coeff = coeff + product[:8] + product[8:]
        coeff = coeff + jnp.dot(part_high, low, preferred_element_type=F32)

    stacked = jnp.concatenate(
        [coeff[:, t * NODES : (t + 1) * NODES] for t in range(TL)], axis=0
    )
    stacked_high = stacked.astype(BF16)
    stacked_low = (stacked - stacked_high.astype(F32)).astype(BF16)
    far = jnp.dot(stacked_high, basis_h[...], preferred_element_type=F32)
    far = far + jnp.dot(stacked_low, basis_h[...], preferred_element_type=F32)
    far = far + jnp.dot(stacked_high, basis_l[...], preferred_element_type=F32)
    for t in range(TL):
        out[t] = far[t * 8 : (t + 1) * 8, :]

    def list_target(t, count):
        box = [coords[d, i * TL + t] for d in range(3)]
        for s in range(SL):
            step = [coords[d, j * SL + s] - box[d] for d in range(3)]
            close = jnp.maximum(jnp.maximum(jnp.abs(step[0]), jnp.abs(step[1])), jnp.abs(step[2])) <= 1
            pairs[count] = t + 8 * s + 128 * (step[0] + 1) + 512 * ((step[1] + 1) * 3 + step[2] + 1)
            count = count + close.astype(jnp.int32)
        return count

    count = lax.fori_loop(0, TL, list_target, 0)
    fetch.wait()

    def near_pair(n, carry):
        code = pairs[n]
        t = jnp.bitwise_and(code, 7)
        s = jnp.bitwise_and(lax.shift_right_logical(code, 3), 15)
        step = jnp.bitwise_and(lax.shift_right_logical(code, 7), 3)
        which = lax.shift_right_logical(code, 9)
        for value in (0, 1, 2):

            @pl.when(step == value)
            def _():
                left = qb[s]
                total = [out[t, :, x * 128 : (x + 1) * 128] for x in range(8)]
                for chunk in range(4 if value == 1 else 8):
                    product = jnp.dot(
                        left,
                        table[which, :, chunk * 256 : (chunk + 1) * 256],
                        preferred_element_type=F32,
                    )
                    for half in range(2):
                        delta = 2 * chunk + half
                        for sx in range(8):
                            if value == 1:
                                hits = {sx - delta, sx + delta}
                            elif value == 2:
                                hits = {8 + sx - delta}
                            else:
                                hits = {delta - 8 + sx}
                            for x in sorted(hits):
                                if 0 <= x < 8:
                                    total[x] = total[x] + product[
                                        sx * 8 : (sx + 1) * 8, half * 128 : (half + 1) * 128
                                    ]
                for x in range(8):
                    out[t, :, x * 128 : (x + 1) * 128] = total[x]

        return carry

    lax.fori_loop(0, count, near_pair, 0)


def local_part(leaf_coords, charges, inverse):
    table = basis_table()
    high, low = split_two(table)
    basis_m = np.concatenate([high, low], axis=1)
    offsets = node_offsets()
    node_sub = np.broadcast_to(offsets[:, :, None], (3, NODES, 128)).astype(np.float32)
    node_lane = np.tile(offsets, (1, TL))
    vmem = pl.BlockSpec(memory_space=pltpu.VMEM)
    return pl.pallas_call(
        local_kernel,
        out_shape=jax.ShapeDtypeStruct((TL, SCEN, LEAF), F32),
        in_specs=[pl.BlockSpec(memory_space=pltpu.SMEM)]
        + [vmem] * 7
        + [pl.BlockSpec(memory_space=pl.ANY)],
        out_specs=vmem,
        scratch_shapes=[
            pltpu.VMEM((9, 128, 2048), BF16),
            pltpu.VMEM((SL, 64, 128), F32),
            pltpu.VMEM((SL, 64, 128), BF16),
            pltpu.SMEM((136,), jnp.int32),
            pltpu.SemaphoreType.DMA,
        ],
        compiler_params=pltpu.CompilerParams(vmem_limit_bytes=40 << 20),
        name="local_part",
    )(
        leaf_coords,
        charges,
        inverse,
        jnp.asarray(basis_m),
        jnp.asarray(np.ascontiguousarray(high.T)),
        jnp.asarray(np.ascontiguousarray(low.T)),
        jnp.asarray(node_sub),
        jnp.asarray(node_lane),
        jnp.asarray(near_table()),
    )


def reduce_kernel(
    part_ref, sq_ref, order_ref, w_ref, basis_ref, pot_ref, root_ref, recv, buf, send_a, recv_a, send_b, recv_b
):
    a = lax.axis_index("tgt")
    b = lax.axis_index("src")
    barrier = pltpu.get_barrier_semaphore()

    def greet(k, carry):
        pl.semaphore_signal(barrier, 1, device_id=(a, lax.rem(b + k, NS)), device_id_type=MESH)
        return carry

    lax.fori_loop(1, NS, greet, 0)
    buf[b] = sq_ref[...]
    pl.semaphore_wait(barrier, NS - 1)

    def square_copy(k):
        return pltpu.make_async_remote_copy(
            src_ref=buf.at[b],
            dst_ref=buf.at[b],
            send_sem=send_b.at[k],
            recv_sem=recv_b.at[b],
            device_id=(a, lax.rem(b + k, NS)),
            device_id_type=MESH,
        )

    def part_copy(k):
        at = lax.rem(b + k, NS)
        return pltpu.make_async_remote_copy(
            src_ref=part_ref.at[at],
            dst_ref=recv.at[b],
            send_sem=send_a.at[k],
            recv_sem=recv_a.at[b],
            device_id=(a, at),
            device_id_type=MESH,
        )

    def start(copy):
        def step(k, carry):
            copy(k).start()
            return carry

        lax.fori_loop(1, NS, step, 0)

    start(square_copy)
    start(part_copy)
    recv[b] = part_ref[b]

    def square_wait(k, carry):
        slot = lax.rem(b + k, NS)
        pltpu.make_async_remote_copy(
            src_ref=buf.at[b],
            dst_ref=buf.at[slot],
            send_sem=send_b.at[0],
            recv_sem=recv_b.at[slot],
            device_id=(a, b),
            device_id_type=MESH,
        ).wait_recv()
        square_copy(k).wait_send()
        return carry

    lax.fori_loop(1, NS, square_wait, 0)
    square = buf[0]
    for k in range(1, NS):
        square = square + buf[k]
    basis = basis_ref[...]
    scaled = jnp.concatenate(
        [basis[:, k * 128 : (k + 1) * 128] * square[k : k + 1, :] for k in range(8)], axis=1
    )
    gram = lax.dot_general(
        scaled, basis, NT_DIMS, precision=lax.Precision.HIGHEST, preferred_element_type=F32
    )
    lane = lax.broadcasted_iota(jnp.int32, (1, NODES), 1)
    left = [gram[8 * k : 8 * k + 8, :] for k in range(8)]
    scale = np.float32(1.0 / math.sqrt(CELLS))
    for k in range(NODES):
        block, row_at = k // 8, k % 8
        row = left[block][row_at : row_at + 1, :]
        pivot = row[:, k : k + 1]
        root = 1.0 / jnp.sqrt(pivot)
        unit = row * root
        root_ref[k : k + 1, :] = jnp.where(lane >= k, unit * scale, 0.0)
        for m in range(block, 8):
            left[m] = left[m] - (left[m][:, k : k + 1] * root) * unit

    def part_wait(k, carry):
        slot = lax.rem(b + k, NS)
        pltpu.make_async_remote_copy(
            src_ref=part_ref.at[0],
            dst_ref=recv.at[slot],
            send_sem=send_a.at[0],
            recv_sem=recv_a.at[slot],
            device_id=(a, b),
            device_id_type=MESH,
        ).wait_recv()
        part_copy(k).wait_send()
        return carry

    lax.fori_loop(1, NS, part_wait, 0)
    total = recv[0]
    for k in range(1, NS):
        total = total + recv[k]
    blocks = [total[:, k * 128 : (k + 1) * 128] for k in range(8)]
    weights = w_ref[pl.ds(pl.multiple_of(b * 8, 8), 8), :]
    for c in range(8):
        index = jnp.broadcast_to(order_ref[0:1, c * 128 : (c + 1) * 128], (8, 128))
        value = permute_row(blocks, index) * weights[c : c + 1, :]
        pot_ref[:, c * 128 : (c + 1) * 128] = value.astype(BF16)


def reduce_part(part, square, order, weights):
    vmem = pl.BlockSpec(memory_space=pltpu.VMEM)
    basis = jnp.asarray(np.ascontiguousarray(basis_table().T))
    return pl.pallas_call(
        reduce_kernel,
        out_shape=(
            jax.ShapeDtypeStruct((SCEN, LEAF), BF16),
            jax.ShapeDtypeStruct((NODES, NODES), F32),
        ),
        in_specs=[vmem] * 5,
        out_specs=(vmem, vmem),
        scratch_shapes=[
            pltpu.VMEM((NS, SCEN, LEAF), F32),
            pltpu.VMEM((NS, 8, 128), F32),
            pltpu.SemaphoreType.DMA((NS,)),
            pltpu.SemaphoreType.DMA((NS,)),
            pltpu.SemaphoreType.DMA((NS,)),
            pltpu.SemaphoreType.DMA((NS,)),
        ],
        compiler_params=pltpu.CompilerParams(collective_id=1, has_side_effects=True),
        name="reduce_part",
    )(part, square, order, weights, basis)


def shards(charges, weights, cell_order, leaf_coords, near_src):
    weights = weights.reshape(TL * 8, 128)
    inverse, square = exchange(cell_order, weights)
    part = local_part(leaf_coords, charges, inverse)
    return tuple(reduce_part(part, square, cell_order, weights))


def solution(mesh):
    placed = (P(None, "src"), P("tgt"), P(("tgt", "src"), None), P(), P("tgt", None))
    return jax.shard_map(
        shards,
        mesh=mesh,
        in_specs=placed,
        out_specs=(P(None, ("tgt", "src")), P()),
        check_vma=False,
    )
```

time: 688 us -> 56.2 us (0.08)
  the two profiles are of different devices: /device:TPU:6 before, /device:TPU:1 now
where the time goes in v1:
time: 56.2 us; the launch traced here: 55.6 us
  Pallas kernels  42.3 us (75%)
  local copies, waits for them, and re-layouts  12.5 us (22%)
  between operations  0.68 us (1%)
    pallas_call x1, Pallas kernels, reduce_part(): pl.pallas_call(reduce_kernel, out_shape=(jax.ShapeDtypeStruct((SCEN, LEAF...  16.6 us
    pallas_call x1, Pallas kernels, exchange(): pl.pallas_call(exchange_kernel, out_shape=(jax.ShapeDtypeStruct((SL, 8, 1...  15.7 us
    unnamed x22, local copies, waits for them, and re-layouts  12.5 us
    pallas_call x1, Pallas kernels, local_part(): pl.pallas_call(local_kernel, out_shape=jax.ShapeDtypeStruct((TL, SCEN, LE...  10.1 us

profile of v1, /device:TPU:1, one launch (start us, length us, event | category | flops | bytes accessed | tf_op | source)
XLA Modules:
  0.0 55.6 jit_solution(3329716072198631828)
XLA Ops:
  0.6 15.7 %exchange.1 = (s32[16,8,128]{2,1,0:T(8,128)}, f32[8,128]{1,0:T(8,128)}) custom-call(s32[1,1024]{1,0:T(1,128)} %order_ref.3, f32[64,128]{1,0:T(8,128)} %bitcast.1), custom_call_target="tpu_custom_call" | custom-call | tf_op jit(solution)/shard_map/exchange/pallas_call | solution.py:220
  16.3 0.0 copy-start
  16.3 2.3 %copy-done = bf16[9,128,2048]{2,1,0:T(8,128)(2,1)S(1)} copy-done((bf16[9,128,2048]{2,1,0:T(8,128)(2,1)S(1)}, bf16[9,128,2048]{2,1,0:T(8,128)(2,1)}, u32[]{:S(2)}) %copy-start) | copy-done | bytes 4718616
  18.7 0.0 copy-start.2
  18.7 0.9 %copy-done.2 = bf16[8,16384]{1,0:T(8,128)(2,1)S(1)} copy-done((bf16[8,16384]{1,0:T(8,128)(2,1)S(1)}, bf16[8,16384]{1,0:T(8,128)(2,1)}, u32[]{:S(2)}) %copy-start.2) | copy-done | bytes 262168
  19.6 0.0 copy-start.3
  19.6 0.9 %copy-done.3 = bf16[1024,128]{1,0:T(8,128)(2,1)S(1)} copy-done((bf16[1024,128]{1,0:T(8,128)(2,1)S(1)}, bf16[1024,128]{1,0:T(8,128)(2,1)}, u32[]{:S(2)}) %copy-start.3) | copy-done | bytes 262168
  20.6 0.0 copy-start.4
  20.6 0.9 %copy-done.4 = bf16[64,1024]{1,0:T(8,128)(2,1)S(1)} copy-done((bf16[64,1024]{1,0:T(8,128)(2,1)S(1)}, bf16[64,1024]{1,0:T(8,128)(2,1)}, u32[]{:S(2)}) %copy-start.4) | copy-done | bytes 131096
  21.5 0.0 copy-start.5
  21.5 0.9 %copy-done.5 = bf16[64,1024]{1,0:T(8,128)(2,1)S(1)} copy-done((bf16[64,1024]{1,0:T(8,128)(2,1)S(1)}, bf16[64,1024]{1,0:T(8,128)(2,1)}, u32[]{:S(2)}) %copy-start.5) | copy-done | bytes 131096
  22.4 0.0 copy-start.6
  22.4 0.9 %copy-done.6 = f32[3,64,128]{2,1,0:T(8,128)S(1)} copy-done((f32[3,64,128]{2,1,0:T(8,128)S(1)}, f32[3,64,128]{2,1,0:T(8,128)}, u32[]{:S(2)}) %copy-start.6) | copy-done | bytes 98328
  23.3 0.0 copy-start.7
  23.3 0.8 %copy-done.7 = s32[16,8,128]{2,1,0:T(8,128)S(1)} copy-done((s32[16,8,128]{2,1,0:T(8,128)S(1)}, s32[16,8,128]{2,1,0:T(8,128)}, u32[]{:S(2)}) %copy-start.7) | copy-done | bytes 65560
  24.1 0.0 copy-start.8
  24.1 0.7 %copy-done.8 = f32[3,512]{1,0:T(4,128)S(1)} copy-done((f32[3,512]{1,0:T(4,128)S(1)}, f32[3,512]{1,0:T(4,128)}, u32[]{:S(2)}) %copy-start.8) | copy-done | bytes 6168
  24.8 0.7 %copy-done.9 = s32[3,128]{1,0:T(4,128)S(1)} copy-done((s32[3,128]{1,0:T(4,128)S(1)}, s32[3,128]{1,0:T(4,128)}, u32[]{:S(2)}) %copy-start.9) | copy-done | bytes 1560
  25.5 10.1 %local_part.1.part_ref = f32[8,8,1024]{2,1,0:T(8,128)S(1)} custom-call(s32[3,128]{1,0:T(4,128)S(1)} %copy-done.9, bf16[8,16384]{1,0:T(8,128)(2,1)S(1)} %copy-done.2, s32[16,8,128]{2,1,0:T(8,128)S(1)} %copy-done.7, bf16[1024,128]{1,0:T(8,128)(2,1)S(1)} %copy-done.3, bf16[64,1024]{1,0:T(8,128)(2,1)S(1)} %copy-done.5, bf16[64,1024]{1,0:T(8,128)(2,1)S(1)} %copy-done.4, ...), custom_call_target="tpu_custom_call" | custom-call | tf_op jit(solution)/shard_map/local_part/pallas_call | solution.py:390
  35.6 0.0 copy-start.1
  35.6 0.7 %copy-done.1 = f32[8,8,1024]{2,1,0:T(8,128)} copy-done((f32[8,8,1024]{2,1,0:T(8,128)}, f32[8,8,1024]{2,1,0:T(8,128)S(1)}, u32[]{:S(2)}) %copy-start.1) | copy-done | bytes 262168
  36.3 16.6 %reduce_part.1 = (bf16[8,1024]{1,0:T(8,128)(2,1)}, f32[64,64]{1,0:T(8,128)}) custom-call(f32[8,8,1024]{2,1,0:T(8,128)} %copy-done.1, f32[8,128]{1,0:T(8,128)} %get-tuple-element.5.sq_ref, s32[1,1024]{1,0:T(1,128)} %order_ref.3, f32[64,128]{1,0:T(8,128)} %bitcast.2, f32[64,1024]{1,0:T(8,128)} %constant.20.clone.basis_ref), custom_call_target="tpu_custom_call" | custom-call | tf_op jit(solution)/shard_map/reduce_part/pallas_call | solution.py:531
  52.9 1.3 %copy.15 = bf16[8,1024]{1,0:T(8,128)(2,1)} copy(bf16[8,1024]{1,0:T(8,128)(2,1)} %get-tuple-element.8) | data formatting | bytes 32768
  54.2 1.4 %copy.16 = f32[64,64]{1,0:T(8,128)} copy(f32[64,64]{1,0:T(8,128)} %get-tuple-element.9) | data formatting | bytes 32768
  (1 shorter events, 0.0 us)
Async XLA Ops:
  16.3 2.3 %copy-start = (bf16[9,128,2048]{2,1,0:T(8,128)(2,1)S(1)}, bf16[9,128,2048]{2,1,0:T(8,128)(2,1)}, u32[]{:S(2)}) copy-start(bf16[9,128,2048]{2,1,0:T(8,128)(2,1)} %constant.19.clone.table_hbm) | copy-start | bytes 14155780
  18.7 0.9 %copy-start.2 = (bf16[8,16384]{1,0:T(8,128)(2,1)S(1)}, bf16[8,16384]{1,0:T(8,128)(2,1)}, u32[]{:S(2)}) copy-start(bf16[8,16384]{1,0:T(8,128)(2,1)} %charges.1) | copy-start | bytes 786436
  19.6 0.9 %copy-start.3 = (bf16[1024,128]{1,0:T(8,128)(2,1)S(1)}, bf16[1024,128]{1,0:T(8,128)(2,1)}, u32[]{:S(2)}) copy-start(bf16[1024,128]{1,0:T(8,128)(2,1)} %constant.14.clone.basis_m) | copy-start | bytes 786436
  20.6 0.9 %copy-start.4 = (bf16[64,1024]{1,0:T(8,128)(2,1)S(1)}, bf16[64,1024]{1,0:T(8,128)(2,1)}, u32[]{:S(2)}) copy-start(bf16[64,1024]{1,0:T(8,128)(2,1)} %constant.16.clone.basis_l) | copy-start | bytes 393220
  21.5 0.9 %copy-start.5 = (bf16[64,1024]{1,0:T(8,128)(2,1)S(1)}, bf16[64,1024]{1,0:T(8,128)(2,1)}, u32[]{:S(2)}) copy-start(bf16[64,1024]{1,0:T(8,128)(2,1)} %constant.15.clone.basis_h) | copy-start | bytes 393220
  22.4 0.9 %copy-start.6 = (f32[3,64,128]{2,1,0:T(8,128)S(1)}, f32[3,64,128]{2,1,0:T(8,128)}, u32[]{:S(2)}) copy-start(f32[3,64,128]{2,1,0:T(8,128)} %constant.17.clone.node_sub) | copy-start | bytes 294916
  23.3 0.8 %copy-start.7 = (s32[16,8,128]{2,1,0:T(8,128)S(1)}, s32[16,8,128]{2,1,0:T(8,128)}, u32[]{:S(2)}) copy-start(s32[16,8,128]{2,1,0:T(8,128)} %get-tuple-element.4.inv) | copy-start | bytes 196612
  24.1 0.7 %copy-start.8 = (f32[3,512]{1,0:T(4,128)S(1)}, f32[3,512]{1,0:T(4,128)}, u32[]{:S(2)}) copy-start(f32[3,512]{1,0:T(4,128)} %constant.18.clone.node_lane) | copy-start | bytes 18436
  24.8 0.7 %copy-start.9 = (s32[3,128]{1,0:T(4,128)S(1)}, s32[3,128]{1,0:T(4,128)}, u32[]{:S(2)}) copy-start(s32[3,128]{1,0:T(4,128)} %coords.1) | copy-start | bytes 4612
  35.6 0.7 %copy-start.1 = (f32[8,8,1024]{2,1,0:T(8,128)}, f32[8,8,1024]{2,1,0:T(8,128)S(1)}, u32[]{:S(2)}) copy-start(f32[8,8,1024]{2,1,0:T(8,128)S(1)} %local_part.1.part_ref) | copy-start | bytes 786436

commit v2 on v1

v2 whole, which is shorter than its diff:
```python
import math

import jax
import jax.numpy as jnp
import numpy as np
from jax import lax
from jax.experimental import pallas as pl
from jax.experimental.pallas import tpu as pltpu
from jax.sharding import PartitionSpec as P

EDGE = 8
LEAF = 1024
SCEN = 8
LV = 128
NT = 16
NS = 8
TL = LV // NT
SL = LV // NS
NODES = 64
CELLS = LV * LEAF
VMEM = 60 << 20
MESH = pl.DeviceIdType.MESH
F32 = jnp.float32
BF16 = jnp.bfloat16
NT_DIMS = (((1,), (1,)), ((), ()))


def chebyshev_nodes(extent):
    return [
        extent * 0.5 + extent * 0.5 * math.cos((2.0 * a + 1.0) * (math.pi / 8.0)) for a in range(4)
    ]


def lagrange(points, nodes, a):
    factor = 1.0
    for b in range(4):
        if b != a:
            factor = factor * ((points - nodes[b]) * (1.0 / (nodes[a] - nodes[b])))
    return factor


def select_by(index, values):
    out = values[0]
    for k in range(1, len(values)):
        out = jnp.where(index == k, values[k], out)
    return out


def basis_by_plane():
    row = lax.broadcasted_iota(jnp.int32, (16, 128), 0)
    lane = lax.broadcasted_iota(jnp.int32, (16, 128), 1)
    short, tall = chebyshev_nodes(8.0), chebyshev_nodes(16.0)
    y = lax.shift_right_logical(lane, 4).astype(F32) + 0.5
    z = jnp.bitwise_and(lane, 15).astype(F32) + 0.5
    along_y = select_by(lax.shift_right_logical(row, 2), [lagrange(y, short, k) for k in range(4)])
    along_z = select_by(jnp.bitwise_and(row, 3), [lagrange(z, tall, k) for k in range(4)])
    plane = along_y * along_z
    return [
        jnp.concatenate([plane * float(lagrange(x + 0.5, short, a)) for a in range(4)], axis=0)
        for x in range(8)
    ]


def node_offset(index):
    short, tall = chebyshev_nodes(8.0), chebyshev_nodes(16.0)
    return [
        select_by(lax.shift_right_logical(index, 4), short),
        select_by(jnp.bitwise_and(lax.shift_right_logical(index, 2), 3), short),
        select_by(jnp.bitwise_and(index, 3), tall),
    ]


def split_two(value):
    high = value.astype(BF16)
    return high, (value - high.astype(F32)).astype(BF16)


def near_tables(table, table_out, sems):
    row = lax.broadcasted_iota(jnp.int32, (128, 128), 0)
    lane = lax.broadcasted_iota(jnp.int32, (128, 128), 1)
    step_y = lax.shift_right_logical(lane, 4) - lax.shift_right_logical(row, 4)
    step_z = jnp.bitwise_and(lane, 15) - jnp.bitwise_and(row, 15)

    def one(o, carry):
        dy = step_y - 8 * (lax.div(o, 3) - 1)
        dz = step_z - 16 * (lax.rem(o, 3) - 1)
        base = (dy * dy + dz * dz).astype(F32)
        for delta in range(16):
            value = 0.05 * lax.rsqrt(base + float(delta * delta + 1))
            table[o, :, delta * 128 : (delta + 1) * 128] = value.astype(BF16)
        pltpu.make_async_copy(table.at[o], table_out.at[o], sems.at[o]).start()
        return carry

    lax.fori_loop(0, 9, one, 0)


def far_tables(coords, i, j, phi, phi_out, sem):
    lane = lax.broadcasted_iota(jnp.int32, (1, TL * NODES), 1)
    slot = lax.shift_right_logical(lane, 6)
    spacing = (8.0, 8.0, 16.0)
    box_at = [select_by(slot, [coords[d, i * TL + t] for t in range(TL)]) for d in range(3)]
    offset = node_offset(jnp.bitwise_and(lane, 63))
    node_at = [box_at[d].astype(F32) * spacing[d] + offset[d] for d in range(3)]
    source = node_offset(lax.broadcasted_iota(jnp.int32, (NODES, TL * NODES), 0))

    def one(s, carry):
        distance = 1.0
        close = None
        for d in range(3):
            box = coords[d, j * SL + s]
            inside = jnp.abs(box_at[d] - box) <= 1
            close = inside if close is None else close & inside
            between = (node_at[d] - box.astype(F32) * spacing[d]) - source[d]
            distance = distance + between * between
        high, low = split_two(jnp.where(close, 0.0, 0.05) * lax.rsqrt(distance))
        phi[0, s] = high
        phi[1, s] = low
        return carry

    lax.fori_loop(0, SL, one, 0)
    pltpu.make_async_copy(phi, phi_out, sem).start()


def exchange_kernel(
    coords, order_ref, w_ref, inv_ref, sq_ref, table_out, phi_out, mine, buf, table, phi, send_a, recv_a, send_b, recv_b, table_sem, phi_sem
):
    a = lax.axis_index("tgt")
    b = lax.axis_index("src")
    barrier = pltpu.get_barrier_semaphore()
    home = lax.rem(a, 2) * NS + b
    column = lax.div(a, 2)
    loops_back = b == column

    def signal_sender(k, carry):
        pl.semaphore_signal(
            barrier, 1, device_id=(2 * b + lax.div(k, NS), lax.rem(k, NS)), device_id_type=MESH
        )
        return carry

    def signal_peer(k, carry):
        pl.semaphore_signal(barrier, 1, device_id=(lax.rem(a + k, NT), b), device_id_type=MESH)
        return carry

    own_sender = lax.rem(a, 2) * NS + b
    sends_to_me = lax.div(a, 2) == b

    def signal_other(k, carry):
        at = lax.rem(own_sender + k, NT)
        return signal_sender(at, carry)

    @pl.when(jnp.logical_not(sends_to_me))
    def _():
        signal_other(0, 0)

    lax.fori_loop(1, NT, signal_other, 0)
    lax.fori_loop(1, NT, signal_peer, 0)

    rows = lax.broadcasted_iota(jnp.int32, (8, 128), 0)
    lanes = lax.broadcasted_iota(jnp.int32, (8, 128), 1)
    low_rows = lax.broadcasted_iota(jnp.int32, (128, 128), 0)
    weights = w_ref[pl.ds(pl.multiple_of(b * 8, 8), 8), :]
    square = weights * weights
    placed = jnp.zeros((40, 128), F32)
    for c in range(8):
        order = order_ref[0:1, c * 128 : (c + 1) * 128]
        hit = lax.shift_right_logical(jnp.broadcast_to(order, (8, 128)), 7) == rows
        value = jnp.broadcast_to(square[c : c + 1, :], (8, 128))
        first = value.astype(BF16).astype(F32)
        rest = value - first
        second = rest.astype(BF16).astype(F32)
        third = rest - second
        parts = [jnp.full((8, 128), float(c), F32), lanes.astype(F32), first, second, third]
        left = jnp.concatenate([jnp.where(hit, part, 0.0) for part in parts], axis=0)
        low = jnp.broadcast_to(jnp.bitwise_and(order, 127), (128, 128)) == low_rows
        right = jnp.where(low, 1.0, 0.0).astype(BF16)
        placed = placed + lax.dot_general(
            left.astype(BF16), right, NT_DIMS, preferred_element_type=F32
        )
    inverse = (placed[0:8] * 128.0 + placed[8:16]).astype(jnp.int32)
    mine[...] = inverse
    buf[a] = placed[16:24] + placed[24:32] + placed[32:40]

    pl.semaphore_wait(
        barrier, jnp.where(loops_back, 2 * NT - 2, 2 * NT - 1).astype(jnp.int32)
    )

    def order_copy(k):
        at = lax.rem(a + k, NT)
        return pltpu.make_async_remote_copy(
            src_ref=mine,
            dst_ref=inv_ref.at[home],
            send_sem=send_a.at[k],
            recv_sem=recv_a.at[home],
            device_id=(at, column),
            device_id_type=MESH,
        )

    def square_copy(k):
        return pltpu.make_async_remote_copy(
            src_ref=buf.at[a],
            dst_ref=buf.at[a],
            send_sem=send_b.at[k],
            recv_sem=recv_b.at[a],
            device_id=(lax.rem(a + k, NT), b),
            device_id_type=MESH,
        )

    @pl.when(jnp.logical_not(loops_back))
    def _():
        order_copy(0).start()

    @pl.when(loops_back)
    def _():
        inv_ref[home] = inverse

    def start_both(k, carry):
        order_copy(k).start()
        square_copy(k).start()
        return carry

    lax.fori_loop(1, NT, start_both, 0)
    far_tables(coords, a, b, phi, phi_out, phi_sem)
    near_tables(table, table_out, table_sem)

    def order_arrival(slot):
        pltpu.make_async_remote_copy(
            src_ref=mine,
            dst_ref=inv_ref.at[slot],
            send_sem=send_a.at[0],
            recv_sem=recv_a.at[slot],
            device_id=(a, b),
            device_id_type=MESH,
        ).wait_recv()

    def square_arrival(slot):
        pltpu.make_async_remote_copy(
            src_ref=mine,
            dst_ref=buf.at[slot],
            send_sem=send_b.at[0],
            recv_sem=recv_b.at[slot],
            device_id=(a, b),
            device_id_type=MESH,
        ).wait_recv()

    @pl.when(jnp.logical_not(loops_back))
    def _():
        order_arrival(home)
        order_copy(0).wait_send()

    def wait_both(k, carry):
        order_arrival(lax.rem(home + k, NT))
        square_arrival(lax.rem(a + k, NT))
        order_copy(k).wait_send()
        square_copy(k).wait_send()
        return carry

    lax.fori_loop(1, NT, wait_both, 0)
    total = buf[0]
    for k in range(1, NT):
        total = total + buf[k]
    sq_ref[...] = total
    pltpu.make_async_copy(phi, phi_out, phi_sem).wait()
    for o in range(9):
        pltpu.make_async_copy(table.at[o], table_out.at[o], table_sem.at[o]).wait()


def exchange(coords, order, weights):
    vmem = pl.BlockSpec(memory_space=pltpu.VMEM)
    hbm = pl.BlockSpec(memory_space=pltpu.HBM)
    return pl.pallas_call(
        exchange_kernel,
        out_shape=(
            jax.ShapeDtypeStruct((SL, 8, 128), jnp.int32),
            jax.ShapeDtypeStruct((8, 128), F32),
            jax.ShapeDtypeStruct((9, 128, 2048), BF16),
            jax.ShapeDtypeStruct((2, SL, NODES, TL * NODES), BF16),
        ),
        in_specs=[pl.BlockSpec(memory_space=pltpu.SMEM), vmem, vmem],
        out_specs=(vmem, vmem, hbm, hbm),
        scratch_shapes=[
            pltpu.VMEM((8, 128), jnp.int32),
            pltpu.VMEM((NT, 8, 128), F32),
            pltpu.VMEM((9, 128, 2048), BF16),
            pltpu.VMEM((2, SL, NODES, TL * NODES), BF16),
            pltpu.SemaphoreType.DMA((NT,)),
            pltpu.SemaphoreType.DMA((NT,)),
            pltpu.SemaphoreType.DMA((NT,)),
            pltpu.SemaphoreType.DMA((NT,)),
            pltpu.SemaphoreType.DMA((9,)),
            pltpu.SemaphoreType.DMA,
        ],
        compiler_params=pltpu.CompilerParams(
            collective_id=0, has_side_effects=True, vmem_limit_bytes=VMEM
        ),
        name="exchange",
    )(coords, order, weights)


def lane_gather(block, lane):
    return jnp.take_along_axis(block, lane, axis=1, mode="promise_in_bounds")


def permute_row(blocks, index):
    block = lax.shift_right_logical(index, 7)
    lane = jnp.bitwise_and(index, 127)
    out = lane_gather(blocks[0], lane)
    for k in range(1, 8):
        out = jnp.where(block == k, lane_gather(blocks[k], lane), out)
    return out


def local_kernel(
    coords, charges_hbm, inv_hbm, table_hbm, phi_hbm, out, charges, inv, table, phi, qf, qb, pairs, counts, sems
):
    i = lax.axis_index("tgt")
    j = lax.axis_index("src")
    fetches = [
        pltpu.make_async_copy(source, target, sems.at[k])
        for k, (source, target) in enumerate(
            [(charges_hbm, charges), (inv_hbm, inv), (phi_hbm, phi), (table_hbm, table)]
        )
    ]
    for fetch in fetches:
        fetch.start()

    def list_target(t, carry):
        box = [coords[d, i * TL + t] for d in range(3)]
        for s in range(SL):
            step = [coords[d, j * SL + s] - box[d] for d in range(3)]
            close = jnp.maximum(jnp.maximum(jnp.abs(step[0]), jnp.abs(step[1])), jnp.abs(step[2])) <= 1
            row = jnp.clip(step[0] + 1, 0, 2)
            count = counts[row]
            pairs[row, count] = t + 8 * s + 256 * ((step[1] + 1) * 3 + step[2] + 1)
            counts[row] = count + close.astype(jnp.int32)
        return carry

    for k in range(3):
        counts[k] = 0
    lax.fori_loop(0, TL, list_target, 0)
    for k in range(3):
        pairs[k, counts[k]] = 8 * SL
    qb[SL] = jnp.zeros((64, 128), BF16)

    fetches[0].wait()
    fetches[1].wait()

    def canonical(leaf, carry):
        base = pl.multiple_of(leaf * LEAF, LEAF)
        raw = charges[:, pl.ds(base, LEAF)].astype(F32)
        blocks = [raw[:, k * 128 : (k + 1) * 128] for k in range(8)]
        order = inv[leaf]
        pieces = [
            permute_row(blocks, jnp.broadcast_to(order[x : x + 1, :], (8, 128))) for x in range(8)
        ]
        rows = jnp.concatenate(pieces, axis=0)
        qf[leaf] = rows
        qb[leaf] = rows.astype(BF16)
        return carry

    lax.fori_loop(0, SL, canonical, 0)

    basis = [split_two(plane) for plane in basis_by_plane()]
    moments = jnp.zeros((SL * SCEN, NODES), F32)
    for x in range(8):
        rows = qf[:, x * 8 : (x + 1) * 8, :].reshape(SL * SCEN, 128).astype(BF16)
        for part in basis[x]:
            moments = moments + lax.dot_general(rows, part, NT_DIMS, preferred_element_type=F32)

    fetches[2].wait()
    coeff = jnp.zeros((SCEN, TL * NODES), F32)
    for s in range(SL):
        high, low = phi[0, s], phi[1, s]
        part_high, part_low = split_two(moments[s * 8 : (s + 1) * 8, :])
        twice = jnp.concatenate([part_high.astype(F32), part_low.astype(F32)], axis=0).astype(BF16)
        product = jnp.dot(twice, high, preferred_element_type=F32)
        coeff = coeff + product[:8] + product[8:]
        coeff = coeff + jnp.dot(part_high, low, preferred_element_type=F32)

    stacked = jnp.concatenate(
        [coeff[:, t * NODES : (t + 1) * NODES] for t in range(TL)], axis=0
    )
    stacked_high, stacked_low = split_two(stacked)
    for x in range(8):
        high, low = basis[x]
        far = jnp.dot(stacked_high, high, preferred_element_type=F32)
        far = far + jnp.dot(stacked_low, high, preferred_element_type=F32)
        far = far + jnp.dot(stacked_high, low, preferred_element_type=F32)
        for t in range(TL):
            out[t, :, x * 128 : (x + 1) * 128] = far[t * 8 : (t + 1) * 8, :]

    fetches[3].wait()

    def near_pairs(value):
        def contribution(code):
            s = jnp.bitwise_and(lax.shift_right_logical(code, 3), 31)
            which = lax.shift_right_logical(code, 8)
            left = qb[s]
            total = [None] * 8
            for chunk in range(4 if value == 1 else 8):
                product = jnp.dot(
                    left,
                    table[which, :, chunk * 256 : (chunk + 1) * 256],
                    preferred_element_type=F32,
                )
                for half in range(2):
                    delta = 2 * chunk + half
                    for sx in range(8):
                        piece = product[sx * 8 : (sx + 1) * 8, half * 128 : (half + 1) * 128]
                        if value == 1:
                            hits = {sx - delta, sx + delta}
                        elif value == 2:
                            hits = {8 + sx - delta}
                        else:
                            hits = {delta - 8 + sx}
                        for x in sorted(hits):
                            if 0 <= x < 8:
                                total[x] = piece if total[x] is None else total[x] + piece
            return total

        def two(n, carry):
            codes = [pairs[value, 2 * n], pairs[value, 2 * n + 1]]
            totals = [contribution(code) for code in codes]
            for code, total in zip(codes, totals):
                t = jnp.bitwise_and(code, 7)
                for x in range(8):
                    out[t, :, x * 128 : (x + 1) * 128] += total[x]
            return carry

        lax.fori_loop(0, lax.shift_right_logical(counts[value] + 1, 1), two, 0)

    for value in range(3):
        near_pairs(value)


def local_part(leaf_coords, charges, inverse, table, phi):
    hbm = pl.BlockSpec(memory_space=pltpu.HBM)
    return pl.pallas_call(
        local_kernel,
        out_shape=jax.ShapeDtypeStruct((TL, SCEN, LEAF), F32),
        in_specs=[pl.BlockSpec(memory_space=pltpu.SMEM)] + [hbm] * 4,
        out_specs=pl.BlockSpec(memory_space=pltpu.VMEM),
        scratch_shapes=[
            pltpu.VMEM((SCEN, SL * LEAF), BF16),
            pltpu.VMEM((SL, 8, 128), jnp.int32),
            pltpu.VMEM((9, 128, 2048), BF16),
            pltpu.VMEM((2, SL, NODES, TL * NODES), BF16),
            pltpu.VMEM((SL, 64, 128), F32),
            pltpu.VMEM((SL + 1, 64, 128), BF16),
            pltpu.SMEM((3, 136), jnp.int32),
            pltpu.SMEM((8,), jnp.int32),
            pltpu.SemaphoreType.DMA((4,)),
        ],
        compiler_params=pltpu.CompilerParams(vmem_limit_bytes=VMEM),
        name="local_part",
    )(leaf_coords, charges, inverse, table, phi)


def cholesky(gram, root_ref):
    full = (8, NODES)
    lane = lax.broadcasted_iota(jnp.int32, full, 1)
    row_at = lax.broadcasted_iota(jnp.int32, full, 0)
    left = [gram[8 * k : 8 * k + 8, :] for k in range(8)]
    scale = 1.0 / math.sqrt(CELLS)
    for kb in range(8):
        base = 8 * kb
        rows = [jnp.broadcast_to(left[kb][r : r + 1, :], full) for r in range(8)]
        cols = [
            [jnp.broadcast_to(left[m][:, base + q : base + q + 1], full) for q in range(8)]
            for m in range(kb, 8)
        ]
        splat = [
            [jnp.broadcast_to(cols[0][q][r : r + 1, :], full) if q >= r else None for q in range(8)]
            for r in range(8)
        ]
        out = jnp.zeros(full, F32)
        for r in range(8):
            root = lax.rsqrt(splat[r][r])
            inverse = root * root
            for q in range(r + 1, 8):
                factor = splat[r][q] * inverse
                for p in range(q, 8):
                    splat[q][p] = splat[q][p] - factor * splat[r][p]
                rows[q] = rows[q] - factor * rows[r]
                for m in range(1, len(cols)):
                    cols[m][q] = cols[m][q] - factor * cols[m][r]
            here = (row_at == r) & (lane >= base + r)
            out = jnp.where(here, rows[r] * (root * scale), out)
            for m in range(1, len(cols)):
                left[kb + m] = left[kb + m] - cols[m][r] * (rows[r] * inverse)
        root_ref[base : base + 8, :] = out


def reduce_kernel(
    part_ref, sq_ref, order_ref, w_ref, pot_ref, root_ref, recv, buf, send_a, recv_a, send_b, recv_b, own_sem
):
    a = lax.axis_index("tgt")
    b = lax.axis_index("src")
    barrier = pltpu.get_barrier_semaphore()

    def greet(k, carry):
        pl.semaphore_signal(barrier, 1, device_id=(a, lax.rem(b + k, NS)), device_id_type=MESH)
        return carry

    lax.fori_loop(1, NS, greet, 0)
    buf[b] = sq_ref[...]
    pl.semaphore_wait(barrier, NS - 1)

    def square_copy(k):
        return pltpu.make_async_remote_copy(
            src_ref=buf.at[b],
            dst_ref=buf.at[b],
            send_sem=send_b.at[k],
            recv_sem=recv_b.at[b],
            device_id=(a, lax.rem(b + k, NS)),
            device_id_type=MESH,
        )

    def part_copy(k):
        at = lax.rem(b + k, NS)
        return pltpu.make_async_remote_copy(
            src_ref=part_ref.at[at],
            dst_ref=recv.at[b],
            send_sem=send_a.at[k],
            recv_sem=recv_a.at[b],
            device_id=(a, at),
            device_id_type=MESH,
        )

    def start(copy):
        def step(k, carry):
            copy(k).start()
            return carry

        lax.fori_loop(1, NS, step, 0)

    start(square_copy)
    start(part_copy)
    own_copy = pltpu.make_async_copy(part_ref.at[b], recv.at[b], own_sem)
    own_copy.start()
    planes = basis_by_plane()

    def square_wait(k, carry):
        slot = lax.rem(b + k, NS)
        pltpu.make_async_remote_copy(
            src_ref=buf.at[b],
            dst_ref=buf.at[slot],
            send_sem=send_b.at[0],
            recv_sem=recv_b.at[slot],
            device_id=(a, b),
            device_id_type=MESH,
        ).wait_recv()
        square_copy(k).wait_send()
        return carry

    lax.fori_loop(1, NS, square_wait, 0)
    square = buf[0]
    for k in range(1, NS):
        square = square + buf[k]
    basis = jnp.concatenate(planes, axis=1)
    scaled = jnp.concatenate([planes[k] * square[k : k + 1, :] for k in range(8)], axis=1)
    gram = lax.dot_general(
        scaled, basis, NT_DIMS, precision=lax.Precision.HIGHEST, preferred_element_type=F32
    )
    cholesky(gram, root_ref)

    def part_wait(k, carry):
        slot = lax.rem(b + k, NS)
        pltpu.make_async_remote_copy(
            src_ref=part_ref.at[0],
            dst_ref=recv.at[slot],
            send_sem=send_a.at[0],
            recv_sem=recv_a.at[slot],
            device_id=(a, b),
            device_id_type=MESH,
        ).wait_recv()
        part_copy(k).wait_send()
        return carry

    own_copy.wait()
    lax.fori_loop(1, NS, part_wait, 0)
    total = recv[0]
    for k in range(1, NS):
        total = total + recv[k]
    blocks = [total[:, k * 128 : (k + 1) * 128] for k in range(8)]
    weights = w_ref[pl.ds(pl.multiple_of(b * 8, 8), 8), :]
    for c in range(8):
        index = jnp.broadcast_to(order_ref[0:1, c * 128 : (c + 1) * 128], (8, 128))
        value = permute_row(blocks, index) * weights[c : c + 1, :]
        pot_ref[:, c * 128 : (c + 1) * 128] = value.astype(BF16)


def reduce_part(part, square, order, weights):
    vmem = pl.BlockSpec(memory_space=pltpu.VMEM)
    return pl.pallas_call(
        reduce_kernel,
        out_shape=(
            jax.ShapeDtypeStruct((SCEN, LEAF), BF16),
            jax.ShapeDtypeStruct((NODES, NODES), F32),
        ),
        in_specs=[pl.BlockSpec(memory_space=pltpu.HBM)] + [vmem] * 3,
        out_specs=(vmem, vmem),
        scratch_shapes=[
            pltpu.VMEM((NS, SCEN, LEAF), F32),
            pltpu.VMEM((NS, 8, 128), F32),
            pltpu.SemaphoreType.DMA((NS,)),
            pltpu.SemaphoreType.DMA((NS,)),
            pltpu.SemaphoreType.DMA((NS,)),
            pltpu.SemaphoreType.DMA((NS,)),
            pltpu.SemaphoreType.DMA,
        ],
        compiler_params=pltpu.CompilerParams(
            collective_id=1, has_side_effects=True, vmem_limit_bytes=VMEM
        ),
        name="reduce_part",
    )(part, square, order, weights)


def shards(charges, weights, cell_order, leaf_coords, near_src):
    weights = weights.reshape(TL * 8, 128)
    inverse, square, table, phi = exchange(leaf_coords, cell_order, weights)
    part = local_part(leaf_coords, charges, inverse, table, phi)
    return tuple(reduce_part(part, square, cell_order, weights))


def solution(mesh):
    placed = (P(None, "src"), P("tgt"), P(("tgt", "src"), None), P(), P("tgt", None))
    return jax.shard_map(
        shards,
        mesh=mesh,
        in_specs=placed,
        out_specs=(P(None, ("tgt", "src")), P()),
        check_vma=False,
    )
```

time: 56.2 us -> 39.9 us (0.71)
  local copies, waits for them, and re-layouts: 12.5 us -> 2.7 us
  Pallas kernels: 42.3 us -> 36.1 us
    unnamed x22 -> x2, local copies, waits for them, and re-layouts: 12.5 us -> 2.7 us
    pallas_call x1, Pallas kernels: 16.6 us -> 11.4 us  [reduce_part(): pl.pallas_call(reduce_kernel, out_shape=(jax.ShapeDtypeStruct((SCEN, LEAF...]
    pallas_call x1, Pallas kernels: 10.1 us -> 8.66 us  [local_part(): pl.pallas_call(local_kernel, out_shape=jax.ShapeDtypeStruct((TL, SCEN, LE...]
where the time goes in v2:
time: 39.9 us; the launch traced here: 39.5 us
  Pallas kernels  36.1 us (90%)
  local copies, waits for them, and re-layouts  2.7 us (7%)
  between operations  0.65 us (2%)
    pallas_call x1, Pallas kernels, exchange(): pl.pallas_call(exchange_kernel, out_shape=(jax.ShapeDtypeStruct((SL, 8, 1...  16.1 us
    pallas_call x1, Pallas kernels, reduce_part(): pl.pallas_call(reduce_kernel, out_shape=(jax.ShapeDtypeStruct((SCEN, LEAF...  11.4 us
    pallas_call x1, Pallas kernels, local_part(): pl.pallas_call(local_kernel, out_shape=jax.ShapeDtypeStruct((TL, SCEN, LE...  8.66 us
    unnamed x2, local copies, waits for them, and re-layouts  2.7 us

profile of v2, /device:TPU:1, one launch (start us, length us, event | category | flops | bytes accessed | tf_op | source)
XLA Modules:
  0.0 39.5 jit_solution(5333331424389536696)
XLA Ops:
  0.6 16.1 %exchange.1 = (s32[16,8,128]{2,1,0:T(8,128)}, f32[8,128]{1,0:T(8,128)}, bf16[9,128,2048]{2,1,0:T(8,128)(2,1)}, bf16[2,16,64,512]{3,2,1,0:T(8,128)(2,1)}) custom-call(s32[3,128]{1,0:T(4,128)} %coords.3, s32[1,1024]{1,0:T(1,128)} %order_ref.3, f32[64,128]{1,0:T(8,128)} %bitcast.1), custom_call_target="tpu_custom_call" | custom-call | tf_op jit(solution)/shard_map/exchange/pallas_call | solution.py:270
  16.7 8.7 %local_part.1.part_ref = f32[8,8,1024]{2,1,0:T(8,128)} custom-call(s32[3,128]{1,0:T(4,128)} %coords.3, bf16[8,16384]{1,0:T(8,128)(2,1)} %charges_hbm.1, s32[16,8,128]{2,1,0:T(8,128)} %get-tuple-element.6.inv_hbm, bf16[9,128,2048]{2,1,0:T(8,128)(2,1)} %get-tuple-element.7.table_hbm, bf16[2,16,64,512]{3,2,1,0:T(8,128)(2,1)} %get-tuple-element.8.phi_hbm), custom_call_target="tpu_custom_call" | custom-call | tf_op jit(solution)/shard_map/local_part/pallas_call | solution.py:437
  25.4 11.4 %reduce_part.1 = (bf16[8,1024]{1,0:T(8,128)(2,1)}, f32[64,64]{1,0:T(8,128)}) custom-call(f32[8,8,1024]{2,1,0:T(8,128)} %local_part.1.part_ref, f32[8,128]{1,0:T(8,128)} %get-tuple-element.9.sq_ref, s32[1,1024]{1,0:T(1,128)} %order_ref.3, f32[64,128]{1,0:T(8,128)} %bitcast.2), custom_call_target="tpu_custom_call" | custom-call | tf_op jit(solution)/shard_map/reduce_part/pallas_call | solution.py:594
  36.8 1.3 %copy.8 = bf16[8,1024]{1,0:T(8,128)(2,1)} copy(bf16[8,1024]{1,0:T(8,128)(2,1)} %get-tuple-element.12) | data formatting | bytes 32768
  38.1 1.4 %copy.9 = f32[64,64]{1,0:T(8,128)} copy(f32[64,64]{1,0:T(8,128)} %get-tuple-element.13) | data formatting | bytes 32768

commit v3 on v2

--- a/solution.py
+++ b/solution.py
@@ -122,7 +122,9 @@
 
 
 def exchange_kernel(
-    coords, order_ref, w_ref, inv_ref, sq_ref, table_out, phi_out, mine, buf, table, phi, send_a, recv_a, send_b, recv_b, table_sem, phi_sem
+    coords_hbm, order_hbm, w_hbm, inv_ref, sq_ref, table_out, phi_out,
+    coords, order_ref, w_ref, mine, buf, table, phi,
+    send_a, recv_a, send_b, recv_b, table_sem, phi_sem, in_sem, own_sem, sq_sem,
 ):
     a = lax.axis_index("tgt")
     b = lax.axis_index("src")
@@ -155,10 +157,20 @@
     lax.fori_loop(1, NT, signal_other, 0)
     lax.fori_loop(1, NT, signal_peer, 0)
 
+    fetches = [
+        pltpu.make_async_copy(order_hbm, order_ref, in_sem.at[0]),
+        pltpu.make_async_copy(w_hbm.at[pl.ds(pl.multiple_of(b * 8, 8), 8)], w_ref, in_sem.at[1]),
+        pltpu.make_async_copy(coords_hbm, coords, in_sem.at[2]),
+    ]
+    for fetch in fetches:
+        fetch.start()
+    for fetch in fetches:
+        fetch.wait()
+
     rows = lax.broadcasted_iota(jnp.int32, (8, 128), 0)
     lanes = lax.broadcasted_iota(jnp.int32, (8, 128), 1)
     low_rows = lax.broadcasted_iota(jnp.int32, (128, 128), 0)
-    weights = w_ref[pl.ds(pl.multiple_of(b * 8, 8), 8), :]
+    weights = w_ref[...]
     square = weights * weights
     placed = jnp.zeros((40, 128), F32)
     for c in range(8):
@@ -209,9 +221,11 @@
     def _():
         order_copy(0).start()
 
+    own_copy = pltpu.make_async_copy(mine, inv_ref.at[home], own_sem)
+
     @pl.when(loops_back)
     def _():
-        inv_ref[home] = inverse
+        own_copy.start()
 
     def start_both(k, carry):
         order_copy(k).start()
@@ -254,18 +268,25 @@
         square_copy(k).wait_send()
         return carry
 
+    @pl.when(loops_back)
+    def _():
+        own_copy.wait()
+
     lax.fori_loop(1, NT, wait_both, 0)
     total = buf[0]
     for k in range(1, NT):
         total = total + buf[k]
-    sq_ref[...] = total
+    mine_sq = buf.at[NT]
+    mine_sq[...] = total
+    sq_copy = pltpu.make_async_copy(mine_sq, sq_ref, sq_sem)
+    sq_copy.start()
+    sq_copy.wait()
     pltpu.make_async_copy(phi, phi_out, phi_sem).wait()
     for o in range(9):
         pltpu.make_async_copy(table.at[o], table_out.at[o], table_sem.at[o]).wait()
 
 
 def exchange(coords, order, weights):
-    vmem = pl.BlockSpec(memory_space=pltpu.VMEM)
     hbm = pl.BlockSpec(memory_space=pltpu.HBM)
     return pl.pallas_call(
         exchange_kernel,
@@ -275,11 +296,14 @@
             jax.ShapeDtypeStruct((9, 128, 2048), BF16),
             jax.ShapeDtypeStruct((2, SL, NODES, TL * NODES), BF16),
         ),
-        in_specs=[pl.BlockSpec(memory_space=pltpu.SMEM), vmem, vmem],
-        out_specs=(vmem, vmem, hbm, hbm),
+        in_specs=[hbm] * 3,
+        out_specs=(hbm,) * 4,
         scratch_shapes=[
+            pltpu.SMEM((3, LV), jnp.int32),
+            pltpu.VMEM((1, LEAF), jnp.int32),
+            pltpu.VMEM((8, 128), F32),
             pltpu.VMEM((8, 128), jnp.int32),
-            pltpu.VMEM((NT, 8, 128), F32),
+            pltpu.VMEM((NT + 1, 8, 128), F32),
             pltpu.VMEM((9, 128, 2048), BF16),
             pltpu.VMEM((2, SL, NODES, TL * NODES), BF16),
             pltpu.SemaphoreType.DMA((NT,)),
@@ -287,6 +311,9 @@
             pltpu.SemaphoreType.DMA((NT,)),
             pltpu.SemaphoreType.DMA((NT,)),
             pltpu.SemaphoreType.DMA((9,)),
+            pltpu.SemaphoreType.DMA,
+            pltpu.SemaphoreType.DMA((3,)),
+            pltpu.SemaphoreType.DMA,
             pltpu.SemaphoreType.DMA,
         ],
         compiler_params=pltpu.CompilerParams(
@@ -380,13 +407,13 @@
         [coeff[:, t * NODES : (t + 1) * NODES] for t in range(TL)], axis=0
     )
     stacked_high, stacked_low = split_two(stacked)
-    for x in range(8):
-        high, low = basis[x]
-        far = jnp.dot(stacked_high, high, preferred_element_type=F32)
-        far = far + jnp.dot(stacked_low, high, preferred_element_type=F32)
-        far = far + jnp.dot(stacked_high, low, preferred_element_type=F32)
-        for t in range(TL):
-            out[t, :, x * 128 : (x + 1) * 128] = far[t * 8 : (t + 1) * 8, :]
+    left = jnp.concatenate([stacked_high, stacked_low, stacked_high], axis=1)
+    right = jnp.concatenate(
+        [jnp.concatenate([basis[x][k] for x in range(8)], axis=1) for k in (0, 0, 1)], axis=0
+    )
+    far = jnp.dot(left, right, preferred_element_type=F32)
+    for t in range(TL):
+        out[t] = far[t * 8 : (t + 1) * 8, :]
 
     fetches[3].wait()
 
@@ -490,9 +517,7 @@
         root_ref[base : base + 8, :] = out
 
 
-def reduce_kernel(
-    part_ref, sq_ref, order_ref, w_ref, pot_ref, root_ref, recv, buf, send_a, recv_a, send_b, recv_b, own_sem
-):
+def reduce_kernel(part_ref, sq_hbm, recv, root_out, buf, root, send_a, recv_a, send_b, recv_b, own_sem):
     a = lax.axis_index("tgt")
     b = lax.axis_index("src")
     barrier = pltpu.get_barrier_semaphore()
@@ -502,7 +527,11 @@
         return carry
 
     lax.fori_loop(1, NS, greet, 0)
-    buf[b] = sq_ref[...]
+    sq_copy = pltpu.make_async_copy(sq_hbm, buf.at[b], own_sem.at[0])
+    own_copy = pltpu.make_async_copy(part_ref.at[b], recv.at[b], own_sem.at[1])
+    sq_copy.start()
+    own_copy.start()
+    sq_copy.wait()
     pl.semaphore_wait(barrier, NS - 1)
 
     def square_copy(k):
@@ -535,8 +564,6 @@
 
     start(square_copy)
     start(part_copy)
-    own_copy = pltpu.make_async_copy(part_ref.at[b], recv.at[b], own_sem)
-    own_copy.start()
     planes = basis_by_plane()
 
     def square_wait(k, carry):
@@ -561,7 +588,9 @@
     gram = lax.dot_general(
         scaled, basis, NT_DIMS, precision=lax.Precision.HIGHEST, preferred_element_type=F32
     )
-    cholesky(gram, root_ref)
+    cholesky(gram, root)
+    root_copy = pltpu.make_async_copy(root, root_out, own_sem.at[2])
+    root_copy.start()
 
     def part_wait(k, carry):
         slot = lax.rem(b + k, NS)
@@ -578,6 +607,37 @@
 
     own_copy.wait()
     lax.fori_loop(1, NS, part_wait, 0)
+    root_copy.wait()
+
+
+def reduce_part(part, square):
+    hbm = pl.BlockSpec(memory_space=pltpu.HBM)
+    return pl.pallas_call(
+        reduce_kernel,
+        out_shape=(
+            jax.ShapeDtypeStruct((NS, SCEN, LEAF), F32),
+            jax.ShapeDtypeStruct((NODES, NODES), F32),
+        ),
+        in_specs=[hbm] * 2,
+        out_specs=(hbm,) * 2,
+        scratch_shapes=[
+            pltpu.VMEM((NS, 8, 128), F32),
+            pltpu.VMEM((NODES, NODES), F32),
+            pltpu.SemaphoreType.DMA((NS,)),
+            pltpu.SemaphoreType.DMA((NS,)),
+            pltpu.SemaphoreType.DMA((NS,)),
+            pltpu.SemaphoreType.DMA((NS,)),
+            pltpu.SemaphoreType.DMA((3,)),
+        ],
+        compiler_params=pltpu.CompilerParams(
+            collective_id=1, has_side_effects=True, vmem_limit_bytes=VMEM
+        ),
+        name="reduce_part",
+    )(part, square)
+
+
+def finish_kernel(recv, root, order_ref, w_ref, pot_ref, root_ref):
+    b = lax.axis_index("src")
     total = recv[0]
     for k in range(1, NS):
         total = total + recv[k]
@@ -587,39 +647,30 @@
         index = jnp.broadcast_to(order_ref[0:1, c * 128 : (c + 1) * 128], (8, 128))
         value = permute_row(blocks, index) * weights[c : c + 1, :]
         pot_ref[:, c * 128 : (c + 1) * 128] = value.astype(BF16)
-
-
-def reduce_part(part, square, order, weights):
+    root_ref[...] = root[...]
+
+
+def finish(recv, root, order, weights):
     vmem = pl.BlockSpec(memory_space=pltpu.VMEM)
     return pl.pallas_call(
-        reduce_kernel,
+        finish_kernel,
         out_shape=(
             jax.ShapeDtypeStruct((SCEN, LEAF), BF16),
             jax.ShapeDtypeStruct((NODES, NODES), F32),
         ),
-        in_specs=[pl.BlockSpec(memory_space=pltpu.HBM)] + [vmem] * 3,
+        in_specs=[vmem] * 4,
         out_specs=(vmem, vmem),
-        scratch_shapes=[
-            pltpu.VMEM((NS, SCEN, LEAF), F32),
-            pltpu.VMEM((NS, 8, 128), F32),
-            pltpu.SemaphoreType.DMA((NS,)),
-            pltpu.SemaphoreType.DMA((NS,)),
-            pltpu.SemaphoreType.DMA((NS,)),
-            pltpu.SemaphoreType.DMA((NS,)),
-            pltpu.SemaphoreType.DMA,
-        ],
-        compiler_params=pltpu.CompilerParams(
-            collective_id=1, has_side_effects=True, vmem_limit_bytes=VMEM
-        ),
-        name="reduce_part",
-    )(part, square, order, weights)
+        compiler_params=pltpu.CompilerParams(vmem_limit_bytes=VMEM),
+        name="finish",
+    )(recv, root, order, weights)
 
 
 def shards(charges, weights, cell_order, leaf_coords, near_src):
     weights = weights.reshape(TL * 8, 128)
     inverse, square, table, phi = exchange(leaf_coords, cell_order, weights)
     part = local_part(leaf_coords, charges, inverse, table, phi)
-    return tuple(reduce_part(part, square, cell_order, weights))
+    recv, root = reduce_part(part, square)
+    return tuple(finish(recv, root, cell_order, weights))
 
 
 def solution(mesh):

time: 39.9 us -> 36.9 us (0.925)
  local copies, waits for them, and re-layouts: 2.7 us -> 0 us
    unnamed x2 -> x0, local copies, waits for them, and re-layouts: 2.7 us -> none
    pallas_call x1, Pallas kernels: 8.66 us -> 9.4 us  [local_part(): pl.pallas_call(local_kernel, out_shape=jax.ShapeDtypeStruct((TL, SCEN, LE...]
    pallas_call x1, Pallas kernels: 16.1 us -> 15.4 us  [exchange(): pl.pallas_call(exchange_kernel, out_shape=(jax.ShapeDtypeStruct((SL, 8, 1...]
    pallas_call x1 -> x2, Pallas kernels: 11.4 us -> 11.2 us  [the longest x1 9.45 us: reduce_part(): pl.pallas_call(reduce_kernel, out_shape=(jax.ShapeDtypeStruct((NS, SCEN,...]
where the time goes in v3:
time: 36.9 us; the launch traced here: 36.7 us
  Pallas kernels  36.1 us (98%)
  between operations  0.65 us (2%)
    pallas_call x1, Pallas kernels, exchange(): pl.pallas_call(exchange_kernel, out_shape=(jax.ShapeDtypeStruct((SL, 8, 1...  15.4 us
    pallas_call x1, Pallas kernels, reduce_part(): pl.pallas_call(reduce_kernel, out_shape=(jax.ShapeDtypeStruct((NS, SCEN,...  9.45 us
    pallas_call x1, Pallas kernels, local_part(): pl.pallas_call(local_kernel, out_shape=jax.ShapeDtypeStruct((TL, SCEN, LE...  9.4 us
    pallas_call x1, Pallas kernels, finish(): pl.pallas_call(finish_kernel, out_shape=(jax.ShapeDtypeStruct((SCEN, LEAF...  1.77 us

profile of v3, /device:TPU:1, one launch (start us, length us, event | category | flops | bytes accessed | tf_op | source)
XLA Modules:
  0.0 36.7 jit_solution(10094986373395114834)
XLA Ops:
  0.6 15.4 %exchange.1 = (s32[16,8,128]{2,1,0:T(8,128)}, f32[8,128]{1,0:T(8,128)}, bf16[9,128,2048]{2,1,0:T(8,128)(2,1)}, bf16[2,16,64,512]{3,2,1,0:T(8,128)(2,1)}) custom-call(s32[3,128]{1,0:T(4,128)} %coords.1, s32[1,1024]{1,0:T(1,128)} %order_ref.1, f32[64,128]{1,0:T(8,128)} %bitcast.1), custom_call_target="tpu_custom_call" | custom-call | tf_op jit(solution)/shard_map/exchange/pallas_call | solution.py:291
  16.1 9.4 %local_part.1.part_ref = f32[8,8,1024]{2,1,0:T(8,128)} custom-call(s32[3,128]{1,0:T(4,128)} %coords.1, bf16[8,16384]{1,0:T(8,128)(2,1)} %charges_hbm.1, s32[16,8,128]{2,1,0:T(8,128)} %get-tuple-element.8.inv_hbm, bf16[9,128,2048]{2,1,0:T(8,128)(2,1)} %get-tuple-element.9.table_hbm, bf16[2,16,64,512]{3,2,1,0:T(8,128)(2,1)} %get-tuple-element.10.phi_hbm), custom_call_target="tpu_custom_call" | custom-call | tf_op jit(solution)/shard_map/local_part/pallas_call | solution.py:464
  25.5 9.5 %reduce_part.1 = (f32[8,8,1024]{2,1,0:T(8,128)}, f32[64,64]{1,0:T(8,128)}) custom-call(f32[8,8,1024]{2,1,0:T(8,128)} %local_part.1.part_ref, f32[8,128]{1,0:T(8,128)} %get-tuple-element.11.sq_hbm), custom_call_target="tpu_custom_call" | custom-call | tf_op jit(solution)/shard_map/reduce_part/pallas_call | solution.py:615
  34.9 1.8 %finish.1 = (bf16[8,1024]{1,0:T(8,128)(2,1)}, f32[64,64]{1,0:T(8,128)}) custom-call(f32[8,8,1024]{2,1,0:T(8,128)} %get-tuple-element.12.recv, f32[64,64]{1,0:T(8,128)} %get-tuple-element.13.root, s32[1,1024]{1,0:T(1,128)} %order_ref.1, f32[64,128]{1,0:T(8,128)} %bitcast.2), custom_call_target="tpu_custom_call" | custom-call | tf_op jit(solution)/shard_map/finish/pallas_call | solution.py:655

commit v4 on v3

--- a/solution.py
+++ b/solution.py
@@ -121,10 +121,43 @@
     pltpu.make_async_copy(phi, phi_out, sem).start()
 
 
+def pair_lists(coords, i, j):
+    lane = lax.broadcasted_iota(jnp.int32, (1, 128), 1)
+    t, s = lax.shift_right_logical(lane, 4), jnp.bitwise_and(lane, 15)
+    step = [
+        select_by(s, [coords[d, j * SL + k] for k in range(SL)])
+        - select_by(t, [coords[d, i * TL + k] for k in range(TL)])
+        for d in range(3)
+    ]
+    close = (jnp.abs(step[0]) <= 1) & (jnp.abs(step[1]) <= 1) & (jnp.abs(step[2]) <= 1)
+    row = lax.broadcasted_iota(jnp.int32, (8, 128), 0)
+    member = jnp.where(jnp.broadcast_to(jnp.where(close, step[0] + 1, 9), (8, 128)) == row, 1.0, 0.0)
+    ahead = lax.broadcasted_iota(jnp.int32, (128, 128), 0) < lax.broadcasted_iota(jnp.int32, (128, 128), 1)
+    rank = jnp.dot(
+        member.astype(BF16), jnp.where(ahead, 1.0, 0.0).astype(BF16), preferred_element_type=F32
+    )
+    place = jnp.full((1, 128), 511.0, F32)
+    for v in range(3):
+        place = jnp.where(member[v : v + 1, :] > 0.5, rank[v : v + 1, :] + float(136 * v), place)
+    position = lax.broadcasted_iota(jnp.int32, (512, 128), 0)
+    spread = jnp.where(jnp.broadcast_to(place.astype(jnp.int32), (512, 128)) == position, 1.0, 0.0)
+    parts = [t + 8 * s, (step[1] + 1) * 3 + step[2] + 1, jnp.full((1, 128), 1, jnp.int32)]
+    left = select_by(row, [jnp.broadcast_to(part, (8, 128)) for part in parts]).astype(F32)
+    listed = lax.dot_general(
+        left.astype(BF16), spread.astype(BF16), NT_DIMS, preferred_element_type=F32
+    ).astype(jnp.int32)
+    out = jnp.where(listed[2:3, :] > 0, listed[0:1, :] + 256 * listed[1:2, :], 8 * SL)
+    at = lax.broadcasted_iota(jnp.int32, (1, 512), 1)
+    for v in range(3):
+        length = jnp.sum(member[v : v + 1, :], axis=1, keepdims=True).astype(jnp.int32)
+        out = jnp.where(at == 408 + v, length, out)
+    return out
+
+
 def exchange_kernel(
-    coords_hbm, order_hbm, w_hbm, inv_ref, sq_ref, table_out, phi_out,
-    coords, order_ref, w_ref, mine, buf, table, phi,
-    send_a, recv_a, send_b, recv_b, table_sem, phi_sem, in_sem, own_sem, sq_sem,
+    coords_hbm, order_hbm, w_hbm, block_ref, table_out, phi_out, list_out,
+    coords, order_ref, w_ref, mine, table, phi, lists,
+    send_a, recv_a, table_sem, phi_sem, in_sem, own_sem, list_sem,
 ):
     a = lax.axis_index("tgt")
     b = lax.axis_index("src")
@@ -134,29 +167,17 @@
     loops_back = b == column
 
     def signal_sender(k, carry):
+        at = lax.rem(home + k, NT)
         pl.semaphore_signal(
-            barrier, 1, device_id=(2 * b + lax.div(k, NS), lax.rem(k, NS)), device_id_type=MESH
+            barrier, 1, device_id=(2 * b + lax.div(at, NS), lax.rem(at, NS)), device_id_type=MESH
         )
         return carry
 
-    def signal_peer(k, carry):
-        pl.semaphore_signal(barrier, 1, device_id=(lax.rem(a + k, NT), b), device_id_type=MESH)
-        return carry
-
-    own_sender = lax.rem(a, 2) * NS + b
-    sends_to_me = lax.div(a, 2) == b
-
-    def signal_other(k, carry):
-        at = lax.rem(own_sender + k, NT)
-        return signal_sender(at, carry)
-
-    @pl.when(jnp.logical_not(sends_to_me))
+    @pl.when(jnp.logical_not(loops_back))
     def _():
-        signal_other(0, 0)
-
-    lax.fori_loop(1, NT, signal_other, 0)
-    lax.fori_loop(1, NT, signal_peer, 0)
-
+        signal_sender(0, 0)
+
+    lax.fori_loop(1, NT, signal_sender, 0)
     fetches = [
         pltpu.make_async_copy(order_hbm, order_ref, in_sem.at[0]),
         pltpu.make_async_copy(w_hbm.at[pl.ds(pl.multiple_of(b * 8, 8), 8)], w_ref, in_sem.at[1]),
@@ -170,8 +191,7 @@
     rows = lax.broadcasted_iota(jnp.int32, (8, 128), 0)
     lanes = lax.broadcasted_iota(jnp.int32, (8, 128), 1)
     low_rows = lax.broadcasted_iota(jnp.int32, (128, 128), 0)
-    weights = w_ref[...]
-    square = weights * weights
+    square = w_ref[...] * w_ref[...]
     placed = jnp.zeros((40, 128), F32)
     for c in range(8):
         order = order_ref[0:1, c * 128 : (c + 1) * 128]
@@ -188,102 +208,72 @@
         placed = placed + lax.dot_general(
             left.astype(BF16), right, NT_DIMS, preferred_element_type=F32
         )
-    inverse = (placed[0:8] * 128.0 + placed[8:16]).astype(jnp.int32)
-    mine[...] = inverse
-    buf[a] = placed[16:24] + placed[24:32] + placed[32:40]
-
-    pl.semaphore_wait(
-        barrier, jnp.where(loops_back, 2 * NT - 2, 2 * NT - 1).astype(jnp.int32)
-    )
-
-    def order_copy(k):
-        at = lax.rem(a + k, NT)
+    mine[0:8, :] = placed[0:8] * 128.0 + placed[8:16]
+    mine[8:16, :] = placed[16:24] + placed[24:32] + placed[32:40]
+
+    pl.semaphore_wait(barrier, jnp.where(loops_back, NT - 1, NT).astype(jnp.int32))
+
+    def block_copy(k):
         return pltpu.make_async_remote_copy(
             src_ref=mine,
-            dst_ref=inv_ref.at[home],
+            dst_ref=block_ref.at[home],
             send_sem=send_a.at[k],
             recv_sem=recv_a.at[home],
-            device_id=(at, column),
+            device_id=(lax.rem(a + k, NT), column),
             device_id_type=MESH,
         )
 
-    def square_copy(k):
-        return pltpu.make_async_remote_copy(
-            src_ref=buf.at[a],
-            dst_ref=buf.at[a],
-            send_sem=send_b.at[k],
-            recv_sem=recv_b.at[a],
-            device_id=(lax.rem(a + k, NT), b),
-            device_id_type=MESH,
-        )
+    def start_block(k, carry):
+        block_copy(k).start()
+        return carry
+
+    lax.fori_loop(1, NT, start_block, 0)
 
     @pl.when(jnp.logical_not(loops_back))
     def _():
-        order_copy(0).start()
-
-    own_copy = pltpu.make_async_copy(mine, inv_ref.at[home], own_sem)
+        block_copy(0).start()
+
+    own_copy = pltpu.make_async_copy(mine, block_ref.at[home], own_sem)
 
     @pl.when(loops_back)
     def _():
         own_copy.start()
 
-    def start_both(k, carry):
-        order_copy(k).start()
-        square_copy(k).start()
-        return carry
-
-    lax.fori_loop(1, NT, start_both, 0)
+    lists[...] = pair_lists(coords, a, b)
+    list_copy = pltpu.make_async_copy(lists, list_out, list_sem)
+    list_copy.start()
     far_tables(coords, a, b, phi, phi_out, phi_sem)
     near_tables(table, table_out, table_sem)
-
-    def order_arrival(slot):
+    list_copy.wait()
+    pltpu.make_async_copy(phi, phi_out, phi_sem).wait()
+    for o in range(9):
+        pltpu.make_async_copy(table.at[o], table_out.at[o], table_sem.at[o]).wait()
+
+    def block_arrival(slot):
         pltpu.make_async_remote_copy(
             src_ref=mine,
-            dst_ref=inv_ref.at[slot],
+            dst_ref=block_ref.at[slot],
             send_sem=send_a.at[0],
             recv_sem=recv_a.at[slot],
             device_id=(a, b),
             device_id_type=MESH,
         ).wait_recv()
 
-    def square_arrival(slot):
-        pltpu.make_async_remote_copy(
-            src_ref=mine,
-            dst_ref=buf.at[slot],
-            send_sem=send_b.at[0],
-            recv_sem=recv_b.at[slot],
-            device_id=(a, b),
-            device_id_type=MESH,
-        ).wait_recv()
-
     @pl.when(jnp.logical_not(loops_back))
     def _():
-        order_arrival(home)
-        order_copy(0).wait_send()
-
-    def wait_both(k, carry):
-        order_arrival(lax.rem(home + k, NT))
-        square_arrival(lax.rem(a + k, NT))
-        order_copy(k).wait_send()
-        square_copy(k).wait_send()
-        return carry
+        block_arrival(home)
+        block_copy(0).wait_send()
 
     @pl.when(loops_back)
     def _():
         own_copy.wait()
 
-    lax.fori_loop(1, NT, wait_both, 0)
-    total = buf[0]
-    for k in range(1, NT):
-        total = total + buf[k]
-    mine_sq = buf.at[NT]
-    mine_sq[...] = total
-    sq_copy = pltpu.make_async_copy(mine_sq, sq_ref, sq_sem)
-    sq_copy.start()
-    sq_copy.wait()
-    pltpu.make_async_copy(phi, phi_out, phi_sem).wait()
-    for o in range(9):
-        pltpu.make_async_copy(table.at[o], table_out.at[o], table_sem.at[o]).wait()
+    def wait_block(k, carry):
+        block_arrival(lax.rem(home + k, NT))
+        block_copy(k).wait_send()
+        return carry
+
+    lax.fori_loop(1, NT, wait_block, 0)
 
 
 def exchange(coords, order, weights):
@@ -291,10 +281,10 @@
     return pl.pallas_call(
         exchange_kernel,
         out_shape=(
-            jax.ShapeDtypeStruct((SL, 8, 128), jnp.int32),
-            jax.ShapeDtypeStruct((8, 128), F32),
+            jax.ShapeDtypeStruct((SL, 16, 128), F32),
             jax.ShapeDtypeStruct((9, 128, 2048), BF16),
             jax.ShapeDtypeStruct((2, SL, NODES, TL * NODES), BF16),
+            jax.ShapeDtypeStruct((1, 512), jnp.int32),
         ),
         in_specs=[hbm] * 3,
         out_specs=(hbm,) * 4,
@@ -302,12 +292,10 @@
             pltpu.SMEM((3, LV), jnp.int32),
             pltpu.VMEM((1, LEAF), jnp.int32),
             pltpu.VMEM((8, 128), F32),
-            pltpu.VMEM((8, 128), jnp.int32),
-            pltpu.VMEM((NT + 1, 8, 128), F32),
+            pltpu.VMEM((16, 128), F32),
             pltpu.VMEM((9, 128, 2048), BF16),
             pltpu.VMEM((2, SL, NODES, TL * NODES), BF16),
-            pltpu.SemaphoreType.DMA((NT,)),
-            pltpu.SemaphoreType.DMA((NT,)),
+            pltpu.VMEM((1, 512), jnp.int32),
             pltpu.SemaphoreType.DMA((NT,)),
             pltpu.SemaphoreType.DMA((NT,)),
             pltpu.SemaphoreType.DMA((9,)),
@@ -337,35 +325,17 @@
 
 
 def local_kernel(
-    coords, charges_hbm, inv_hbm, table_hbm, phi_hbm, out, charges, inv, table, phi, qf, qb, pairs, counts, sems
+    charges_hbm, block_hbm, table_hbm, phi_hbm, list_hbm, out, sq_out,
+    charges, block, table, phi, qf, qb, pairs, sems,
 ):
-    i = lax.axis_index("tgt")
-    j = lax.axis_index("src")
     fetches = [
         pltpu.make_async_copy(source, target, sems.at[k])
         for k, (source, target) in enumerate(
-            [(charges_hbm, charges), (inv_hbm, inv), (phi_hbm, phi), (table_hbm, table)]
+            [(charges_hbm, charges), (block_hbm, block), (phi_hbm, phi), (table_hbm, table), (list_hbm, pairs)]
         )
     ]
     for fetch in fetches:
         fetch.start()
-
-    def list_target(t, carry):
-        box = [coords[d, i * TL + t] for d in range(3)]
-        for s in range(SL):
-            step = [coords[d, j * SL + s] - box[d] for d in range(3)]
-            close = jnp.maximum(jnp.maximum(jnp.abs(step[0]), jnp.abs(step[1])), jnp.abs(step[2])) <= 1
-            row = jnp.clip(step[0] + 1, 0, 2)
-            count = counts[row]
-            pairs[row, count] = t + 8 * s + 256 * ((step[1] + 1) * 3 + step[2] + 1)
-            counts[row] = count + close.astype(jnp.int32)
-        return carry
-
-    for k in range(3):
-        counts[k] = 0
-    lax.fori_loop(0, TL, list_target, 0)
-    for k in range(3):
-        pairs[k, counts[k]] = 8 * SL
     qb[SL] = jnp.zeros((64, 128), BF16)
 
     fetches[0].wait()
@@ -375,7 +345,7 @@
         base = pl.multiple_of(leaf * LEAF, LEAF)
         raw = charges[:, pl.ds(base, LEAF)].astype(F32)
         blocks = [raw[:, k * 128 : (k + 1) * 128] for k in range(8)]
-        order = inv[leaf]
+        order = block[leaf, 0:8, :].astype(jnp.int32)
         pieces = [
             permute_row(blocks, jnp.broadcast_to(order[x : x + 1, :], (8, 128))) for x in range(8)
         ]
@@ -384,7 +354,11 @@
         qb[leaf] = rows.astype(BF16)
         return carry
 
-    lax.fori_loop(0, SL, canonical, 0)
+    lax.fori_loop(0, SL, canonical, 0, unroll=4)
+    square = block[0, 8:16, :]
+    for leaf in range(1, SL):
+        square = square + block[leaf, 8:16, :]
+    sq_out[...] = square
 
     basis = [split_two(plane) for plane in basis_by_plane()]
     moments = jnp.zeros((SL * SCEN, NODES), F32)
@@ -416,6 +390,7 @@
         out[t] = far[t * 8 : (t + 1) * 8, :]
 
     fetches[3].wait()
+    fetches[4].wait()
 
     def near_pairs(value):
         def contribution(code):
@@ -445,7 +420,7 @@
             return total
 
         def two(n, carry):
-            codes = [pairs[value, 2 * n], pairs[value, 2 * n + 1]]
+            codes = [pairs[0, 136 * value + 2 * n + k] for k in range(2)]
             totals = [contribution(code) for code in codes]
             for code, total in zip(codes, totals):
                 t = jnp.bitwise_and(code, 7)
@@ -453,33 +428,36 @@
                     out[t, :, x * 128 : (x + 1) * 128] += total[x]
             return carry
 
-        lax.fori_loop(0, lax.shift_right_logical(counts[value] + 1, 1), two, 0)
+        lax.fori_loop(0, lax.shift_right_logical(pairs[0, 408 + value] + 1, 1), two, 0)
 
     for value in range(3):
         near_pairs(value)
 
 
-def local_part(leaf_coords, charges, inverse, table, phi):
+def local_part(charges, block, table, phi, lists):
     hbm = pl.BlockSpec(memory_space=pltpu.HBM)
+    vmem = pl.BlockSpec(memory_space=pltpu.VMEM)
     return pl.pallas_call(
         local_kernel,
-        out_shape=jax.ShapeDtypeStruct((TL, SCEN, LEAF), F32),
-        in_specs=[pl.BlockSpec(memory_space=pltpu.SMEM)] + [hbm] * 4,
-        out_specs=pl.BlockSpec(memory_space=pltpu.VMEM),
+        out_shape=(
+            jax.ShapeDtypeStruct((TL, SCEN, LEAF), F32),
+            jax.ShapeDtypeStruct((8, 128), F32),
+        ),
+        in_specs=[hbm] * 5,
+        out_specs=(vmem, vmem),
         scratch_shapes=[
             pltpu.VMEM((SCEN, SL * LEAF), BF16),
-            pltpu.VMEM((SL, 8, 128), jnp.int32),
+            pltpu.VMEM((SL, 16, 128), F32),
             pltpu.VMEM((9, 128, 2048), BF16),
             pltpu.VMEM((2, SL, NODES, TL * NODES), BF16),
             pltpu.VMEM((SL, 64, 128), F32),
             pltpu.VMEM((SL + 1, 64, 128), BF16),
-            pltpu.SMEM((3, 136), jnp.int32),
-            pltpu.SMEM((8,), jnp.int32),
-            pltpu.SemaphoreType.DMA((4,)),
+            pltpu.SMEM((1, 512), jnp.int32),
+            pltpu.SemaphoreType.DMA((5,)),
         ],
         compiler_params=pltpu.CompilerParams(vmem_limit_bytes=VMEM),
         name="local_part",
-    )(leaf_coords, charges, inverse, table, phi)
+    )(charges, block, table, phi, lists)
 
 
 def cholesky(gram, root_ref):
@@ -667,8 +645,8 @@
 
 def shards(charges, weights, cell_order, leaf_coords, near_src):
     weights = weights.reshape(TL * 8, 128)
-    inverse, square, table, phi = exchange(leaf_coords, cell_order, weights)
-    part = local_part(leaf_coords, charges, inverse, table, phi)
+    block, table, phi, lists = exchange(leaf_coords, cell_order, weights)
+    part, square = local_part(charges, block, table, phi, lists)
     recv, root = reduce_part(part, square)
     return tuple(finish(recv, root, cell_order, weights))
 

time: 36.9 us -> 32.9 us (0.89)
  Pallas kernels: 36.1 us -> 32 us
    pallas_call x2, Pallas kernels: 24.8 us -> 19.2 us  [the longest x1 12.9 us: exchange(): pl.pallas_call(exchange_kernel, out_shape=(jax.ShapeDtypeStruct((SL, 16,...]
    pallas_call x1, Pallas kernels: 9.45 us -> 10.9 us  [reduce_part(): pl.pallas_call(reduce_kernel, out_shape=(jax.ShapeDtypeStruct((NS, SCEN,...]
where the time goes in v4:
time: 32.9 us; the launch traced here: 32.6 us
  Pallas kernels  32 us (97%)
  between operations  0.65 us (2%)
    pallas_call x1, Pallas kernels, exchange(): pl.pallas_call(exchange_kernel, out_shape=(jax.ShapeDtypeStruct((SL, 16,...  12.9 us
    pallas_call x1, Pallas kernels, reduce_part(): pl.pallas_call(reduce_kernel, out_shape=(jax.ShapeDtypeStruct((NS, SCEN,...  10.9 us
    pallas_call x1, Pallas kernels, local_part(): pl.pallas_call(local_kernel, out_shape=(jax.ShapeDtypeStruct((TL, SCEN, L...  6.39 us
    pallas_call x1, Pallas kernels, finish(): pl.pallas_call(finish_kernel, out_shape=(jax.ShapeDtypeStruct((SCEN, LEAF...  1.77 us

profile of v4, /device:TPU:1, one launch (start us, length us, event | category | flops | bytes accessed | tf_op | source)
XLA Modules:
  0.0 32.6 jit_solution(16247969347628710352)
XLA Ops:
  0.6 12.9 %exchange.1 = (f32[16,16,128]{2,1,0:T(8,128)}, bf16[9,128,2048]{2,1,0:T(8,128)(2,1)}, bf16[2,16,64,512]{3,2,1,0:T(8,128)(2,1)}, s32[1,512]{1,0:T(1,128)}) custom-call(s32[3,128]{1,0:T(4,128)} %coords_hbm.1, s32[1,1024]{1,0:T(1,128)} %order_ref.1, f32[64,128]{1,0:T(8,128)} %bitcast.1), custom_call_target="tpu_custom_call" | custom-call | tf_op jit(solution)/shard_map/exchange/pallas_call | solution.py:281
  13.5 6.4 %local_part.1 = (f32[8,8,1024]{2,1,0:T(8,128)}, f32[8,128]{1,0:T(8,128)}) custom-call(bf16[8,16384]{1,0:T(8,128)(2,1)} %charges_hbm.1, f32[16,16,128]{2,1,0:T(8,128)} %get-tuple-element.10.block_hbm, bf16[9,128,2048]{2,1,0:T(8,128)(2,1)} %get-tuple-element.11.table_hbm, bf16[2,16,64,512]{3,2,1,0:T(8,128)(2,1)} %get-tuple-element.12.phi_hbm, ...), custom_call_target="tpu_custom_call" | custom-call | tf_op jit(solution)/shard_map/local_part/pallas_call | solution.py:440
  19.9 10.9 %reduce_part.1 = (f32[8,8,1024]{2,1,0:T(8,128)}, f32[64,64]{1,0:T(8,128)}) custom-call(f32[8,8,1024]{2,1,0:T(8,128)} %get-tuple-element.14.part_ref, f32[8,128]{1,0:T(8,128)} %get-tuple-element.15.sq_hbm), custom_call_target="tpu_custom_call" | custom-call | tf_op jit(solution)/shard_map/reduce_part/pallas_call | solution.py:593
  30.8 1.8 %finish.1 = (bf16[8,1024]{1,0:T(8,128)(2,1)}, f32[64,64]{1,0:T(8,128)}) custom-call(f32[8,8,1024]{2,1,0:T(8,128)} %get-tuple-element.16.recv, f32[64,64]{1,0:T(8,128)} %get-tuple-element.17.root, s32[1,1024]{1,0:T(1,128)} %order_ref.1, f32[64,128]{1,0:T(8,128)} %bitcast.2), custom_call_target="tpu_custom_call" | custom-call | tf_op jit(solution)/shard_map/finish/pallas_call | solution.py:633

commit v5 on v4

--- a/solution.py
+++ b/solution.py
@@ -131,24 +131,24 @@
     ]
     close = (jnp.abs(step[0]) <= 1) & (jnp.abs(step[1]) <= 1) & (jnp.abs(step[2]) <= 1)
     row = lax.broadcasted_iota(jnp.int32, (8, 128), 0)
-    member = jnp.where(jnp.broadcast_to(jnp.where(close, step[0] + 1, 9), (8, 128)) == row, 1.0, 0.0)
+    member = jnp.where(jnp.broadcast_to(jnp.where(close, jnp.where(step[0] == 0, 1, 0), 9), (8, 128)) == row, 1.0, 0.0)
     ahead = lax.broadcasted_iota(jnp.int32, (128, 128), 0) < lax.broadcasted_iota(jnp.int32, (128, 128), 1)
     rank = jnp.dot(
         member.astype(BF16), jnp.where(ahead, 1.0, 0.0).astype(BF16), preferred_element_type=F32
     )
     place = jnp.full((1, 128), 511.0, F32)
-    for v in range(3):
+    for v in range(2):
         place = jnp.where(member[v : v + 1, :] > 0.5, rank[v : v + 1, :] + float(136 * v), place)
     position = lax.broadcasted_iota(jnp.int32, (512, 128), 0)
     spread = jnp.where(jnp.broadcast_to(place.astype(jnp.int32), (512, 128)) == position, 1.0, 0.0)
-    parts = [t + 8 * s, (step[1] + 1) * 3 + step[2] + 1, jnp.full((1, 128), 1, jnp.int32)]
+    parts = [t + 8 * s, (step[1] + 1) * 3 + step[2] + 1, jnp.full((1, 128), 1, jnp.int32), jnp.where(step[0] < 0, 1, 0)]
     left = select_by(row, [jnp.broadcast_to(part, (8, 128)) for part in parts]).astype(F32)
     listed = lax.dot_general(
         left.astype(BF16), spread.astype(BF16), NT_DIMS, preferred_element_type=F32
     ).astype(jnp.int32)
-    out = jnp.where(listed[2:3, :] > 0, listed[0:1, :] + 256 * listed[1:2, :], 8 * SL)
+    out = jnp.where(listed[2:3, :] > 0, listed[0:1, :] + 256 * listed[1:2, :] + 4096 * listed[3:4, :], 8 * SL)
     at = lax.broadcasted_iota(jnp.int32, (1, 512), 1)
-    for v in range(3):
+    for v in range(2):
         length = jnp.sum(member[v : v + 1, :], axis=1, keepdims=True).astype(jnp.int32)
         out = jnp.where(at == 408 + v, length, out)
     return out
@@ -325,18 +325,19 @@
 
 
 def local_kernel(
-    charges_hbm, block_hbm, table_hbm, phi_hbm, list_hbm, out, sq_out,
-    charges, block, table, phi, qf, qb, pairs, sems,
+    charges_hbm, block_hbm, table_hbm, list_hbm, out, moments_out, sq_out,
+    charges, block, table, qf, qb, pairs, sems,
 ):
     fetches = [
         pltpu.make_async_copy(source, target, sems.at[k])
         for k, (source, target) in enumerate(
-            [(charges_hbm, charges), (block_hbm, block), (phi_hbm, phi), (table_hbm, table), (list_hbm, pairs)]
+            [(charges_hbm, charges), (block_hbm, block), (table_hbm, table), (list_hbm, pairs)]
         )
     ]
     for fetch in fetches:
         fetch.start()
     qb[SL] = jnp.zeros((64, 128), BF16)
+    out[...] = jnp.zeros((TL, 8, SCEN, 128), F32)
 
     fetches[0].wait()
     fetches[1].wait()
@@ -352,6 +353,7 @@
         rows = jnp.concatenate(pieces, axis=0)
         qf[leaf] = rows
         qb[leaf] = rows.astype(BF16)
+        qb[SL + 1 + leaf] = jnp.concatenate(pieces[::-1], axis=0).astype(BF16)
         return carry
 
     lax.fori_loop(0, SL, canonical, 0, unroll=4)
@@ -360,43 +362,21 @@
         square = square + block[leaf, 8:16, :]
     sq_out[...] = square
 
-    basis = [split_two(plane) for plane in basis_by_plane()]
     moments = jnp.zeros((SL * SCEN, NODES), F32)
-    for x in range(8):
+    for x, plane in enumerate(basis_by_plane()):
         rows = qf[:, x * 8 : (x + 1) * 8, :].reshape(SL * SCEN, 128).astype(BF16)
-        for part in basis[x]:
+        for part in split_two(plane):
             moments = moments + lax.dot_general(rows, part, NT_DIMS, preferred_element_type=F32)
-
+    moments_out[...] = moments
     fetches[2].wait()
-    coeff = jnp.zeros((SCEN, TL * NODES), F32)
-    for s in range(SL):
-        high, low = phi[0, s], phi[1, s]
-        part_high, part_low = split_two(moments[s * 8 : (s + 1) * 8, :])
-        twice = jnp.concatenate([part_high.astype(F32), part_low.astype(F32)], axis=0).astype(BF16)
-        product = jnp.dot(twice, high, preferred_element_type=F32)
-        coeff = coeff + product[:8] + product[8:]
-        coeff = coeff + jnp.dot(part_high, low, preferred_element_type=F32)
-
-    stacked = jnp.concatenate(
-        [coeff[:, t * NODES : (t + 1) * NODES] for t in range(TL)], axis=0
-    )
-    stacked_high, stacked_low = split_two(stacked)
-    left = jnp.concatenate([stacked_high, stacked_low, stacked_high], axis=1)
-    right = jnp.concatenate(
-        [jnp.concatenate([basis[x][k] for x in range(8)], axis=1) for k in (0, 0, 1)], axis=0
-    )
-    far = jnp.dot(left, right, preferred_element_type=F32)
-    for t in range(TL):
-        out[t] = far[t * 8 : (t + 1) * 8, :]
-
     fetches[3].wait()
-    fetches[4].wait()
 
     def near_pairs(value):
         def contribution(code):
             s = jnp.bitwise_and(lax.shift_right_logical(code, 3), 31)
-            which = lax.shift_right_logical(code, 8)
-            left = qb[s]
+            which = jnp.bitwise_and(lax.shift_right_logical(code, 8), 15)
+            mirrored = lax.shift_right_logical(code, 12)
+            left = qb[s + (SL + 1) * mirrored]
             total = [None] * 8
             for chunk in range(4 if value == 1 else 8):
                 product = jnp.dot(
@@ -408,56 +388,51 @@
                     delta = 2 * chunk + half
                     for sx in range(8):
                         piece = product[sx * 8 : (sx + 1) * 8, half * 128 : (half + 1) * 128]
-                        if value == 1:
-                            hits = {sx - delta, sx + delta}
-                        elif value == 2:
-                            hits = {8 + sx - delta}
-                        else:
-                            hits = {delta - 8 + sx}
-                        for x in sorted(hits):
+                        for x in sorted({sx - delta, sx + delta} if value == 1 else {8 + sx - delta}):
                             if 0 <= x < 8:
                                 total[x] = piece if total[x] is None else total[x] + piece
             return total
 
-        def two(n, carry):
-            codes = [pairs[0, 136 * value + 2 * n + k] for k in range(2)]
+        def four(n, carry):
+            codes = [pairs[0, 136 * value + 4 * n + k] for k in range(4)]
             totals = [contribution(code) for code in codes]
             for code, total in zip(codes, totals):
                 t = jnp.bitwise_and(code, 7)
+                mirrored = lax.shift_right_logical(code, 12)
                 for x in range(8):
-                    out[t, :, x * 128 : (x + 1) * 128] += total[x]
+                    out[t, x if value == 1 else x + mirrored * (7 - 2 * x)] += total[x]
             return carry
 
-        lax.fori_loop(0, lax.shift_right_logical(pairs[0, 408 + value] + 1, 1), two, 0)
-
-    for value in range(3):
+        lax.fori_loop(0, lax.shift_right_logical(pairs[0, 408 + value] + 3, 2), four, 0)
+
+    for value in range(2):
         near_pairs(value)
 
 
-def local_part(charges, block, table, phi, lists):
+def local_part(charges, block, table, lists):
     hbm = pl.BlockSpec(memory_space=pltpu.HBM)
     vmem = pl.BlockSpec(memory_space=pltpu.VMEM)
     return pl.pallas_call(
         local_kernel,
         out_shape=(
-            jax.ShapeDtypeStruct((TL, SCEN, LEAF), F32),
+            jax.ShapeDtypeStruct((TL, 8, SCEN, 128), F32),
+            jax.ShapeDtypeStruct((SL * SCEN, NODES), F32),
             jax.ShapeDtypeStruct((8, 128), F32),
         ),
-        in_specs=[hbm] * 5,
-        out_specs=(vmem, vmem),
+        in_specs=[hbm] * 4,
+        out_specs=(vmem,) * 3,
         scratch_shapes=[
             pltpu.VMEM((SCEN, SL * LEAF), BF16),
             pltpu.VMEM((SL, 16, 128), F32),
             pltpu.VMEM((9, 128, 2048), BF16),
-            pltpu.VMEM((2, SL, NODES, TL * NODES), BF16),
             pltpu.VMEM((SL, 64, 128), F32),
-            pltpu.VMEM((SL + 1, 64, 128), BF16),
+            pltpu.VMEM((2 * SL + 1, 64, 128), BF16),
             pltpu.SMEM((1, 512), jnp.int32),
-            pltpu.SemaphoreType.DMA((5,)),
+            pltpu.SemaphoreType.DMA((4,)),
         ],
         compiler_params=pltpu.CompilerParams(vmem_limit_bytes=VMEM),
         name="local_part",
-    )(charges, block, table, phi, lists)
+    )(charges, block, table, lists)
 
 
 def cholesky(gram, root_ref):
@@ -495,7 +470,10 @@
         root_ref[base : base + 8, :] = out
 
 
-def reduce_kernel(part_ref, sq_hbm, recv, root_out, buf, root, send_a, recv_a, send_b, recv_b, own_sem):
+def reduce_kernel(
+    part_ref, sq_hbm, moments_hbm, phi_hbm, recv, far_recv, root_out,
+    buf, root, moments, phi, coeff, send_a, recv_a, send_b, recv_b, send_c, recv_c, own_sem,
+):
     a = lax.axis_index("tgt")
     b = lax.axis_index("src")
     barrier = pltpu.get_barrier_semaphore()
@@ -508,6 +486,10 @@
     sq_copy = pltpu.make_async_copy(sq_hbm, buf.at[b], own_sem.at[0])
     own_copy = pltpu.make_async_copy(part_ref.at[b], recv.at[b], own_sem.at[1])
     sq_copy.start()
+    moments_copy = pltpu.make_async_copy(moments_hbm, moments, own_sem.at[3])
+    phi_copy = pltpu.make_async_copy(phi_hbm, phi, own_sem.at[4])
+    moments_copy.start()
+    phi_copy.start()
     own_copy.start()
     sq_copy.wait()
     pl.semaphore_wait(barrier, NS - 1)
@@ -542,6 +524,37 @@
 
     start(square_copy)
     start(part_copy)
+
+    moments_copy.wait()
+    phi_copy.wait()
+    found = jnp.zeros((2 * SCEN, TL * NODES), F32)
+    extra = jnp.zeros((SCEN, TL * NODES), F32)
+    for s in range(0, SL, 4):
+        rows = jnp.concatenate([moments[(s + k) * 8 : (s + k + 1) * 8, :] for k in range(4)], axis=1)
+        high = rows.astype(BF16).astype(F32)
+        twice = jnp.concatenate([high, rows - high], axis=0).astype(BF16)
+        couple = [phi[k, s : s + 4].reshape(4 * NODES, TL * NODES) for k in range(2)]
+        found = found + jnp.dot(twice, couple[0], preferred_element_type=F32)
+        extra = extra + jnp.dot(high.astype(BF16), couple[1], preferred_element_type=F32)
+    total = found[:SCEN] + found[SCEN:] + extra
+    for t in range(TL):
+        coeff[t, :, 0:NODES] = total[:, t * NODES : (t + 1) * NODES]
+        coeff[t, :, NODES:128] = jnp.zeros((SCEN, NODES), F32)
+
+    def far_copy(k):
+        at = lax.rem(b + k, NS)
+        return pltpu.make_async_remote_copy(
+            src_ref=coeff.at[at],
+            dst_ref=far_recv.at[b],
+            send_sem=send_c.at[k],
+            recv_sem=recv_c.at[b],
+            device_id=(a, at),
+            device_id_type=MESH,
+        )
+
+    start(far_copy)
+    own_far = pltpu.make_async_copy(coeff.at[b], far_recv.at[b], own_sem.at[5])
+    own_far.start()
     planes = basis_by_plane()
 
     def square_wait(k, carry):
@@ -581,45 +594,68 @@
             device_id_type=MESH,
         ).wait_recv()
         part_copy(k).wait_send()
+        pltpu.make_async_remote_copy(
+            src_ref=coeff.at[0],
+            dst_ref=far_recv.at[slot],
+            send_sem=send_c.at[0],
+            recv_sem=recv_c.at[slot],
+            device_id=(a, b),
+            device_id_type=MESH,
+        ).wait_recv()
+        far_copy(k).wait_send()
         return carry
 
     own_copy.wait()
+    own_far.wait()
     lax.fori_loop(1, NS, part_wait, 0)
     root_copy.wait()
 
 
-def reduce_part(part, square):
+def reduce_part(part, square, moments, phi):
     hbm = pl.BlockSpec(memory_space=pltpu.HBM)
     return pl.pallas_call(
         reduce_kernel,
         out_shape=(
-            jax.ShapeDtypeStruct((NS, SCEN, LEAF), F32),
+            jax.ShapeDtypeStruct((NS, 8, SCEN, 128), F32),
+            jax.ShapeDtypeStruct((NS, SCEN, 128), F32),
             jax.ShapeDtypeStruct((NODES, NODES), F32),
         ),
-        in_specs=[hbm] * 2,
-        out_specs=(hbm,) * 2,
+        in_specs=[hbm] * 4,
+        out_specs=(hbm,) * 3,
         scratch_shapes=[
             pltpu.VMEM((NS, 8, 128), F32),
             pltpu.VMEM((NODES, NODES), F32),
-            pltpu.SemaphoreType.DMA((NS,)),
-            pltpu.SemaphoreType.DMA((NS,)),
-            pltpu.SemaphoreType.DMA((NS,)),
-            pltpu.SemaphoreType.DMA((NS,)),
-            pltpu.SemaphoreType.DMA((3,)),
-        ],
+            pltpu.VMEM((SL * SCEN, NODES), F32),
+            pltpu.VMEM((2, SL, NODES, TL * NODES), BF16),
+            pltpu.VMEM((TL, SCEN, 128), F32),
+        ]
+        + [pltpu.SemaphoreType.DMA((NS,))] * 6
+        + [pltpu.SemaphoreType.DMA((6,))],
         compiler_params=pltpu.CompilerParams(
             collective_id=1, has_side_effects=True, vmem_limit_bytes=VMEM
         ),
         name="reduce_part",
-    )(part, square)
-
-
-def finish_kernel(recv, root, order_ref, w_ref, pot_ref, root_ref):
+    )(part, square, moments, phi)
+
+
+def finish_kernel(recv, far_recv, root, order_ref, w_ref, pot_ref, root_ref):
     b = lax.axis_index("src")
-    total = recv[0]
+    coeff = far_recv[0]
     for k in range(1, NS):
-        total = total + recv[k]
-    blocks = [total[:, k * 128 : (k + 1) * 128] for k in range(8)]
+        coeff = coeff + far_recv[k]
+    high, low = split_two(coeff[:, 0:NODES])
+    left = jnp.concatenate([high, low, high], axis=1)
+    basis = [split_two(plane) for plane in basis_by_plane()]
+    right = jnp.concatenate(
+        [jnp.concatenate([basis[x][k] for x in range(8)], axis=1) for k in (0, 0, 1)], axis=0
+    )
+    far = jnp.dot(left, right, preferred_element_type=F32)
+    blocks = []
+    for x in range(8):
+        total = recv[0, x]
+        for k in range(1, NS):
+            total = total + recv[k, x]
+        blocks.append(total + far[:, x * 128 : (x + 1) * 128])
     weights = w_ref[pl.ds(pl.multiple_of(b * 8, 8), 8), :]
     for c in range(8):
         index = jnp.broadcast_to(order_ref[0:1, c * 128 : (c + 1) * 128], (8, 128))
@@ -628,7 +664,7 @@
     root_ref[...] = root[...]
 
 
-def finish(recv, root, order, weights):
+def finish(recv, far_recv, root, order, weights):
     vmem = pl.BlockSpec(memory_space=pltpu.VMEM)
     return pl.pallas_call(
         finish_kernel,
@@ -636,19 +672,19 @@
             jax.ShapeDtypeStruct((SCEN, LEAF), BF16),
             jax.ShapeDtypeStruct((NODES, NODES), F32),
         ),
-        in_specs=[vmem] * 4,
+        in_specs=[vmem] * 5,
         out_specs=(vmem, vmem),
         compiler_params=pltpu.CompilerParams(vmem_limit_bytes=VMEM),
         name="finish",
-    )(recv, root, order, weights)
+    )(recv, far_recv, root, order, weights)
 
 
 def shards(charges, weights, cell_order, leaf_coords, near_src):
     weights = weights.reshape(TL * 8, 128)
     block, table, phi, lists = exchange(leaf_coords, cell_order, weights)
-    part, square = local_part(charges, block, table, phi, lists)
-    recv, root = reduce_part(part, square)
-    return tuple(finish(recv, root, cell_order, weights))
+    part, moments, square = local_part(charges, block, table, lists)
+    recv, far_recv, root = reduce_part(part, square, moments, phi)
+    return tuple(finish(recv, far_recv, root, cell_order, weights))
 
 
 def solution(mesh):

time: 32.9 us -> 32.8 us (level)
  no operation moved by 1% of the time
where the time goes in v5:
time: 32.8 us; the launch traced here: 32.6 us
  Pallas kernels  32 us (98%)
  between operations  0.65 us (2%)
    pallas_call x1, Pallas kernels, exchange(): pl.pallas_call(exchange_kernel, out_shape=(jax.ShapeDtypeStruct((SL, 16,...  12.9 us
    pallas_call x1, Pallas kernels, reduce_part(): pl.pallas_call(reduce_kernel, out_shape=(jax.ShapeDtypeStruct((NS, 8, SCE...  12.1 us
    pallas_call x1, Pallas kernels, local_part(): pl.pallas_call(local_kernel, out_shape=(jax.ShapeDtypeStruct((TL, 8, SCEN...  5.01 us
    pallas_call x1, Pallas kernels, finish(): pl.pallas_call(finish_kernel, out_shape=(jax.ShapeDtypeStruct((SCEN, LEAF...  2.01 us

profile of v5, /device:TPU:1, one launch (start us, length us, event | category | flops | bytes accessed | tf_op | source)
XLA Modules:
  0.0 32.6 jit_solution(12245056388883697303)
XLA Ops:
  0.6 12.9 %exchange.1 = (f32[16,16,128]{2,1,0:T(8,128)}, bf16[9,128,2048]{2,1,0:T(8,128)(2,1)}, bf16[2,16,64,512]{3,2,1,0:T(8,128)(2,1)}, s32[1,512]{1,0:T(1,128)}) custom-call(s32[3,128]{1,0:T(4,128)} %coords_hbm.1, s32[1,1024]{1,0:T(1,128)} %order_ref.1, f32[64,128]{1,0:T(8,128)} %bitcast.1), custom_call_target="tpu_custom_call" | custom-call | tf_op jit(solution)/shard_map/exchange/pallas_call | solution.py:281
  13.5 5.0 %local_part.1 = (f32[8,8,8,128]{3,2,1,0:T(8,128)}, f32[128,64]{1,0:T(8,128)}, f32[8,128]{1,0:T(8,128)}) custom-call(bf16[8,16384]{1,0:T(8,128)(2,1)} %charges_hbm.1, f32[16,16,128]{2,1,0:T(8,128)} %get-tuple-element.12.block_hbm, bf16[9,128,2048]{2,1,0:T(8,128)(2,1)} %get-tuple-element.13.table_hbm, s32[1,512]{1,0:T(1,128)} %get-tuple-element.14.list_hbm), custom_call_target="tpu_custom_call" | custom-call | tf_op jit(solution)/shard_map/local_part/pallas_call | solution.py:415
  18.5 12.1 %reduce_part.1 = (f32[8,8,8,128]{3,2,1,0:T(8,128)}, f32[8,8,128]{2,1,0:T(8,128)}, f32[64,64]{1,0:T(8,128)}) custom-call(f32[8,8,8,128]{3,2,1,0:T(8,128)} %get-tuple-element.15.part_ref, f32[8,128]{1,0:T(8,128)} %get-tuple-element.16.sq_hbm, f32[128,64]{1,0:T(8,128)} %get-tuple-element.17.moments_hbm, bf16[2,16,64,512]{3,2,1,0:T(8,128)(2,1)} %get-tuple-element.18.phi_hbm), custom_call_target="tpu_custom_call" | custom-call | tf_op jit(solution)/shard_map/reduce_part/pallas_call | solution.py:616
  30.6 2.0 %finish.1 = (bf16[8,1024]{1,0:T(8,128)(2,1)}, f32[64,64]{1,0:T(8,128)}) custom-call(f32[8,8,8,128]{3,2,1,0:T(8,128)} %get-tuple-element.19.recv, f32[8,8,128]{2,1,0:T(8,128)} %get-tuple-element.20.far_recv, f32[64,64]{1,0:T(8,128)} %get-tuple-element.21.root, s32[1,1024]{1,0:T(1,128)} %order_ref.1, f32[64,128]{1,0:T(8,128)} %bitcast.2), custom_call_target="tpu_custom_call" | custom-call | tf_op jit(solution)/shard_map/finish/pallas_call | solution.py:669

commit v6 on v5

--- a/solution.py
+++ b/solution.py
@@ -19,6 +19,7 @@
 NODES = 64
 CELLS = LV * LEAF
 VMEM = 60 << 20
+FAR_FIRST = (4, 3, 5, 2, 6, 1, 7)
 MESH = pl.DeviceIdType.MESH
 F32 = jnp.float32
 BF16 = jnp.bfloat16
@@ -342,21 +343,51 @@
     fetches[0].wait()
     fetches[1].wait()
 
-    def canonical(leaf, carry):
-        base = pl.multiple_of(leaf * LEAF, LEAF)
-        raw = charges[:, pl.ds(base, LEAF)].astype(F32)
+    low_rows = lax.broadcasted_iota(jnp.int16, (128, 128), 0)
+    one = jnp.ones((128, 128), BF16)
+    zero = jnp.zeros((128, 128), BF16)
+
+    def by_gather(raw, order):
         blocks = [raw[:, k * 128 : (k + 1) * 128] for k in range(8)]
-        order = block[leaf, 0:8, :].astype(jnp.int32)
-        pieces = [
+        return [
             permute_row(blocks, jnp.broadcast_to(order[x : x + 1, :], (8, 128))) for x in range(8)
         ]
-        rows = jnp.concatenate(pieces, axis=0)
-        qf[leaf] = rows
-        qb[leaf] = rows.astype(BF16)
-        qb[SL + 1 + leaf] = jnp.concatenate(pieces[::-1], axis=0).astype(BF16)
-        return carry
-
-    lax.fori_loop(0, SL, canonical, 0, unroll=4)
+
+    def by_product(raw, order):
+        left = jnp.concatenate([raw[:, k * 128 : (k + 1) * 128] for k in range(8)], axis=0).astype(BF16)
+        block_at = lax.shift_right_logical(order, 7)
+        low = jnp.bitwise_and(order, 127)
+        pieces = []
+        for x in range(0, 8, 2):
+            hots = [
+                jnp.where(
+                    jnp.broadcast_to(low[y : y + 1, :], (128, 128)).astype(jnp.int16) == low_rows,
+                    one,
+                    zero,
+                )
+                for y in (x, x + 1)
+            ]
+            spread = jnp.dot(left, jnp.concatenate(hots, axis=1), preferred_element_type=F32)
+            for half in range(2):
+                wanted = jnp.broadcast_to(block_at[x + half : x + half + 1, :], (8, 128))
+                lanes = slice(half * 128, (half + 1) * 128)
+                pieces.append(select_by(wanted, [spread[k * 8 : (k + 1) * 8, lanes] for k in range(8)]))
+        return pieces
+
+    def canonical(group, carry):
+        for k in range(4):
+            leaf = group * 4 + k
+            base = pl.multiple_of(leaf * LEAF, LEAF)
+            raw = charges[:, pl.ds(base, LEAF)].astype(F32)
+            order = block[leaf, 0:8, :].astype(jnp.int32)
+            pieces = by_product(raw, order) if k < 2 else by_gather(raw, order)
+            rows = jnp.concatenate(pieces, axis=0)
+            qf[leaf] = rows
+            qb[leaf] = rows.astype(BF16)
+            qb[SL + 1 + leaf] = jnp.concatenate(pieces[::-1], axis=0).astype(BF16)
+        return carry
+
+    lax.fori_loop(0, SL // 4, canonical, 0)
     square = block[0, 8:16, :]
     for leaf in range(1, SL):
         square = square + block[leaf, 8:16, :]
@@ -379,31 +410,41 @@
             left = qb[s + (SL + 1) * mirrored]
             total = [None] * 8
             for chunk in range(4 if value == 1 else 8):
+                first, last = (0, 8) if value == 1 else (max(0, 2 * chunk - 8), min(8, 2 * chunk + 2))
                 product = jnp.dot(
-                    left,
+                    left[first * 8 : last * 8],
                     table[which, :, chunk * 256 : (chunk + 1) * 256],
                     preferred_element_type=F32,
                 )
                 for half in range(2):
                     delta = 2 * chunk + half
-                    for sx in range(8):
-                        piece = product[sx * 8 : (sx + 1) * 8, half * 128 : (half + 1) * 128]
+                    for sx in range(first, last):
+                        piece = product[(sx - first) * 8 : (sx - first + 1) * 8, half * 128 : (half + 1) * 128]
                         for x in sorted({sx - delta, sx + delta} if value == 1 else {8 + sx - delta}):
                             if 0 <= x < 8:
                                 total[x] = piece if total[x] is None else total[x] + piece
             return total
 
-        def four(n, carry):
-            codes = [pairs[0, 136 * value + 4 * n + k] for k in range(4)]
+        def step(first, size):
+            codes = [pairs[0, first + k] for k in range(size)]
             totals = [contribution(code) for code in codes]
             for code, total in zip(codes, totals):
                 t = jnp.bitwise_and(code, 7)
                 mirrored = lax.shift_right_logical(code, 12)
                 for x in range(8):
                     out[t, x if value == 1 else x + mirrored * (7 - 2 * x)] += total[x]
+
+        def eight(n, carry):
+            step(136 * value + 8 * n, 8)
             return carry
 
-        lax.fori_loop(0, lax.shift_right_logical(pairs[0, 408 + value] + 3, 2), four, 0)
+        length = pairs[0, 408 + value]
+        full = lax.shift_right_logical(length + 3, 3)
+        lax.fori_loop(0, full, eight, 0)
+
+        @pl.when(length > 8 * full)
+        def _():
+            step(136 * value + 8 * full, 4)
 
     for value in range(2):
         near_pairs(value)
@@ -453,20 +494,29 @@
             for r in range(8)
         ]
         out = jnp.zeros(full, F32)
-        for r in range(8):
-            root = lax.rsqrt(splat[r][r])
-            inverse = root * root
-            for q in range(r + 1, 8):
-                factor = splat[r][q] * inverse
-                for p in range(q, 8):
-                    splat[q][p] = splat[q][p] - factor * splat[r][p]
-                rows[q] = rows[q] - factor * rows[r]
+        for r in range(0, 8, 2):
+            p, q, w = splat[r][r], splat[r][r + 1], splat[r + 1][r + 1]
+            inverse = lax.rsqrt(p * w - q * q)
+            inverse = inverse * inverse
+            pp, qq, ww = p * inverse, q * inverse, w * inverse
+            for k in range(r + 2, 8):
+                one = splat[r][k] * ww - splat[r + 1][k] * qq
+                two = splat[r + 1][k] * pp - splat[r][k] * qq
+                for m in range(k, 8):
+                    splat[k][m] = splat[k][m] - (one * splat[r][m] + two * splat[r + 1][m])
+                rows[k] = rows[k] - (one * rows[r] + two * rows[r + 1])
                 for m in range(1, len(cols)):
-                    cols[m][q] = cols[m][q] - factor * cols[m][r]
-            here = (row_at == r) & (lane >= base + r)
-            out = jnp.where(here, rows[r] * (root * scale), out)
+                    cols[m][k] = cols[m][k] - (one * cols[m][r] + two * cols[m][r + 1])
+            root = lax.rsqrt(p)
+            ratio = q * (root * root)
+            first = rows[r] * (root * scale)
+            second = (rows[r + 1] - ratio * rows[r]) * (lax.rsqrt(w - ratio * q) * scale)
+            out = jnp.where((row_at == r) & (lane >= base + r), first, out)
+            out = jnp.where((row_at == r + 1) & (lane >= base + r + 1), second, out)
+            above = ww * rows[r] - qq * rows[r + 1]
+            below = pp * rows[r + 1] - qq * rows[r]
             for m in range(1, len(cols)):
-                left[kb + m] = left[kb + m] - cols[m][r] * (rows[r] * inverse)
+                left[kb + m] = left[kb + m] - (cols[m][r] * above + cols[m][r + 1] * below)
         root_ref[base : base + 8, :] = out
 
 
@@ -516,11 +566,8 @@
         )
 
     def start(copy):
-        def step(k, carry):
+        for k in FAR_FIRST:
             copy(k).start()
-            return carry
-
-        lax.fori_loop(1, NS, step, 0)
 
     start(square_copy)
     start(part_copy)

time: 32.8 us -> 31.9 us (0.973)
  Pallas kernels: 32 us -> 30.8 us
    pallas_call x1, Pallas kernels: 12.1 us -> 10.4 us  [reduce_part(): pl.pallas_call(reduce_kernel, out_shape=(jax.ShapeDtypeStruct((NS, 8, SCE...]
    pallas_call x1, Pallas kernels: 5.01 us -> 5.56 us  [local_part(): pl.pallas_call(local_kernel, out_shape=(jax.ShapeDtypeStruct((TL, 8, SCEN...]
where the time goes in v6:
time: 31.9 us; the launch traced here: 31.4 us
  Pallas kernels  30.8 us (97%)
  between operations  0.65 us (2%)
    pallas_call x1, Pallas kernels, exchange(): pl.pallas_call(exchange_kernel, out_shape=(jax.ShapeDtypeStruct((SL, 16,...  12.9 us
    pallas_call x1, Pallas kernels, reduce_part(): pl.pallas_call(reduce_kernel, out_shape=(jax.ShapeDtypeStruct((NS, 8, SCE...  10.4 us
    pallas_call x1, Pallas kernels, local_part(): pl.pallas_call(local_kernel, out_shape=(jax.ShapeDtypeStruct((TL, 8, SCEN...  5.56 us
    pallas_call x1, Pallas kernels, finish(): pl.pallas_call(finish_kernel, out_shape=(jax.ShapeDtypeStruct((SCEN, LEAF...  2.01 us

profile of v6, /device:TPU:1, one launch (start us, length us, event | category | flops | bytes accessed | tf_op | source)
XLA Modules:
  0.0 31.4 jit_solution(14551354130250432896)
XLA Ops:
  0.6 12.9 %exchange.1 = (f32[16,16,128]{2,1,0:T(8,128)}, bf16[9,128,2048]{2,1,0:T(8,128)(2,1)}, bf16[2,16,64,512]{3,2,1,0:T(8,128)(2,1)}, s32[1,512]{1,0:T(1,128)}) custom-call(s32[3,128]{1,0:T(4,128)} %coords_hbm.1, s32[1,1024]{1,0:T(1,128)} %order_ref.1, f32[64,128]{1,0:T(8,128)} %bitcast.1), custom_call_target="tpu_custom_call" | custom-call | tf_op jit(solution)/shard_map/exchange/pallas_call | solution.py:282
  13.5 5.6 %local_part.1 = (f32[8,8,8,128]{3,2,1,0:T(8,128)}, f32[128,64]{1,0:T(8,128)}, f32[8,128]{1,0:T(8,128)}) custom-call(bf16[8,16384]{1,0:T(8,128)(2,1)} %charges_hbm.1, f32[16,16,128]{2,1,0:T(8,128)} %get-tuple-element.12.block_hbm, bf16[9,128,2048]{2,1,0:T(8,128)(2,1)} %get-tuple-element.13.table_hbm, s32[1,512]{1,0:T(1,128)} %get-tuple-element.14.list_hbm), custom_call_target="tpu_custom_call" | custom-call | tf_op jit(solution)/shard_map/local_part/pallas_call | solution.py:456
  19.1 10.4 %reduce_part.1 = (f32[8,8,8,128]{3,2,1,0:T(8,128)}, f32[8,8,128]{2,1,0:T(8,128)}, f32[64,64]{1,0:T(8,128)}) custom-call(f32[8,8,8,128]{3,2,1,0:T(8,128)} %get-tuple-element.15.part_ref, f32[8,128]{1,0:T(8,128)} %get-tuple-element.16.sq_hbm, f32[128,64]{1,0:T(8,128)} %get-tuple-element.17.moments_hbm, bf16[2,16,64,512]{3,2,1,0:T(8,128)(2,1)} %get-tuple-element.18.phi_hbm), custom_call_target="tpu_custom_call" | custom-call | tf_op jit(solution)/shard_map/reduce_part/pallas_call | solution.py:663
  29.4 2.0 %finish.1 = (bf16[8,1024]{1,0:T(8,128)(2,1)}, f32[64,64]{1,0:T(8,128)}) custom-call(f32[8,8,8,128]{3,2,1,0:T(8,128)} %get-tuple-element.19.recv, f32[8,8,128]{2,1,0:T(8,128)} %get-tuple-element.20.far_recv, f32[64,64]{1,0:T(8,128)} %get-tuple-element.21.root, s32[1,1024]{1,0:T(1,128)} %order_ref.1, f32[64,128]{1,0:T(8,128)} %bitcast.2), custom_call_target="tpu_custom_call" | custom-call | tf_op jit(solution)/shard_map/finish/pallas_call | solution.py:716

commit v7 on v6

--- a/solution.py
+++ b/solution.py
@@ -375,19 +375,19 @@
         return pieces
 
     def canonical(group, carry):
-        for k in range(4):
-            leaf = group * 4 + k
+        for k in range(8):
+            leaf = group * 8 + k
             base = pl.multiple_of(leaf * LEAF, LEAF)
             raw = charges[:, pl.ds(base, LEAF)].astype(F32)
             order = block[leaf, 0:8, :].astype(jnp.int32)
-            pieces = by_product(raw, order) if k < 2 else by_gather(raw, order)
+            pieces = by_product(raw, order) if k % 2 == 0 else by_gather(raw, order)
             rows = jnp.concatenate(pieces, axis=0)
             qf[leaf] = rows
             qb[leaf] = rows.astype(BF16)
             qb[SL + 1 + leaf] = jnp.concatenate(pieces[::-1], axis=0).astype(BF16)
         return carry
 
-    lax.fori_loop(0, SL // 4, canonical, 0)
+    lax.fori_loop(0, SL // 8, canonical, 0)
     square = block[0, 8:16, :]
     for leaf in range(1, SL):
         square = square + block[leaf, 8:16, :]

time: 31.9 us -> 32 us (level)
  Pallas kernels: 30.8 us -> 31.2 us
    pallas_call x1, Pallas kernels: 10.4 us -> 11.4 us  [reduce_part(): pl.pallas_call(reduce_kernel, out_shape=(jax.ShapeDtypeStruct((NS, 8, SCE...]
    pallas_call x1, Pallas kernels: 5.56 us -> 4.94 us  [local_part(): pl.pallas_call(local_kernel, out_shape=(jax.ShapeDtypeStruct((TL, 8, SCEN...]
where the time goes in v7:
time: 32 us; the launch traced here: 31.8 us
  Pallas kernels  31.2 us (98%)
  between operations  0.65 us (2%)
    pallas_call x1, Pallas kernels, exchange(): pl.pallas_call(exchange_kernel, out_shape=(jax.ShapeDtypeStruct((SL, 16,...  12.9 us
    pallas_call x1, Pallas kernels, reduce_part(): pl.pallas_call(reduce_kernel, out_shape=(jax.ShapeDtypeStruct((NS, 8, SCE...  11.4 us
    pallas_call x1, Pallas kernels, local_part(): pl.pallas_call(local_kernel, out_shape=(jax.ShapeDtypeStruct((TL, 8, SCEN...  4.94 us
    pallas_call x1, Pallas kernels, finish(): pl.pallas_call(finish_kernel, out_shape=(jax.ShapeDtypeStruct((SCEN, LEAF...  2.01 us

profile of v7, /device:TPU:1, one launch (start us, length us, event | category | flops | bytes accessed | tf_op | source)
XLA Modules:
  0.0 31.8 jit_solution(9488592357087234382)
XLA Ops:
  0.6 12.9 %exchange.1 = (f32[16,16,128]{2,1,0:T(8,128)}, bf16[9,128,2048]{2,1,0:T(8,128)(2,1)}, bf16[2,16,64,512]{3,2,1,0:T(8,128)(2,1)}, s32[1,512]{1,0:T(1,128)}) custom-call(s32[3,128]{1,0:T(4,128)} %coords_hbm.1, s32[1,1024]{1,0:T(1,128)} %order_ref.1, f32[64,128]{1,0:T(8,128)} %bitcast.1), custom_call_target="tpu_custom_call" | custom-call | tf_op jit(solution)/shard_map/exchange/pallas_call | solution.py:282
  13.5 4.9 %local_part.1 = (f32[8,8,8,128]{3,2,1,0:T(8,128)}, f32[128,64]{1,0:T(8,128)}, f32[8,128]{1,0:T(8,128)}) custom-call(bf16[8,16384]{1,0:T(8,128)(2,1)} %charges_hbm.1, f32[16,16,128]{2,1,0:T(8,128)} %get-tuple-element.12.block_hbm, bf16[9,128,2048]{2,1,0:T(8,128)(2,1)} %get-tuple-element.13.table_hbm, s32[1,512]{1,0:T(1,128)} %get-tuple-element.14.list_hbm), custom_call_target="tpu_custom_call" | custom-call | tf_op jit(solution)/shard_map/local_part/pallas_call | solution.py:456
  18.4 11.4 %reduce_part.1 = (f32[8,8,8,128]{3,2,1,0:T(8,128)}, f32[8,8,128]{2,1,0:T(8,128)}, f32[64,64]{1,0:T(8,128)}) custom-call(f32[8,8,8,128]{3,2,1,0:T(8,128)} %get-tuple-element.15.part_ref, f32[8,128]{1,0:T(8,128)} %get-tuple-element.16.sq_hbm, f32[128,64]{1,0:T(8,128)} %get-tuple-element.17.moments_hbm, bf16[2,16,64,512]{3,2,1,0:T(8,128)(2,1)} %get-tuple-element.18.phi_hbm), custom_call_target="tpu_custom_call" | custom-call | tf_op jit(solution)/shard_map/reduce_part/pallas_call | solution.py:663
  29.8 2.0 %finish.1 = (bf16[8,1024]{1,0:T(8,128)(2,1)}, f32[64,64]{1,0:T(8,128)}) custom-call(f32[8,8,8,128]{3,2,1,0:T(8,128)} %get-tuple-element.19.recv, f32[8,8,128]{2,1,0:T(8,128)} %get-tuple-element.20.far_recv, f32[64,64]{1,0:T(8,128)} %get-tuple-element.21.root, s32[1,1024]{1,0:T(1,128)} %order_ref.1, f32[64,128]{1,0:T(8,128)} %bitcast.2), custom_call_target="tpu_custom_call" | custom-call | tf_op jit(solution)/shard_map/finish/pallas_call | solution.py:716

commit v8 on v6

--- a/solution.py
+++ b/solution.py
@@ -19,7 +19,6 @@
 NODES = 64
 CELLS = LV * LEAF
 VMEM = 60 << 20
-FAR_FIRST = (4, 3, 5, 2, 6, 1, 7)
 MESH = pl.DeviceIdType.MESH
 F32 = jnp.float32
 BF16 = jnp.bfloat16
@@ -566,8 +565,12 @@
         )
 
     def start(copy):
-        for k in FAR_FIRST:
-            copy(k).start()
+        def step(n, carry):
+            half = lax.div(n + 1, 2)
+            copy(4 + half * (1 - 2 * lax.rem(n, 2))).start()
+            return carry
+
+        lax.fori_loop(0, NS - 1, step, 0)
 
     start(square_copy)
     start(part_copy)

time: 31.9 us -> 32 us (level); the launches traced: 31.4 us -> 31.9 us
  Pallas kernels: 30.8 us -> 31.3 us
    pallas_call x1, Pallas kernels: 10.4 us -> 11.6 us  [reduce_part(): pl.pallas_call(reduce_kernel, out_shape=(jax.ShapeDtypeStruct((NS, 8, SCE...]
    pallas_call x1, Pallas kernels: 5.56 us -> 4.8 us  [local_part(): pl.pallas_call(local_kernel, out_shape=(jax.ShapeDtypeStruct((TL, 8, SCEN...]
where the time goes in v8:
time: 32 us; the launch traced here: 31.9 us
  Pallas kernels  31.3 us (98%)
  between operations  0.65 us (2%)
    pallas_call x1, Pallas kernels, exchange(): pl.pallas_call(exchange_kernel, out_shape=(jax.ShapeDtypeStruct((SL, 16,...  12.9 us
    pallas_call x1, Pallas kernels, reduce_part(): pl.pallas_call(reduce_kernel, out_shape=(jax.ShapeDtypeStruct((NS, 8, SCE...  11.6 us
    pallas_call x1, Pallas kernels, local_part(): pl.pallas_call(local_kernel, out_shape=(jax.ShapeDtypeStruct((TL, 8, SCEN...  4.8 us
    pallas_call x1, Pallas kernels, finish(): pl.pallas_call(finish_kernel, out_shape=(jax.ShapeDtypeStruct((SCEN, LEAF...  2.01 us

profile of v8, /device:TPU:1, one launch (start us, length us, event | category | flops | bytes accessed | tf_op | source)
XLA Modules:
  0.0 31.9 jit_solution(5464803948908096319)
XLA Ops:
  0.6 12.9 %exchange.1 = (f32[16,16,128]{2,1,0:T(8,128)}, bf16[9,128,2048]{2,1,0:T(8,128)(2,1)}, bf16[2,16,64,512]{3,2,1,0:T(8,128)(2,1)}, s32[1,512]{1,0:T(1,128)}) custom-call(s32[3,128]{1,0:T(4,128)} %coords_hbm.1, s32[1,1024]{1,0:T(1,128)} %order_ref.1, f32[64,128]{1,0:T(8,128)} %bitcast.1), custom_call_target="tpu_custom_call" | custom-call | tf_op jit(solution)/shard_map/exchange/pallas_call | solution.py:281
  13.5 4.8 %local_part.1 = (f32[8,8,8,128]{3,2,1,0:T(8,128)}, f32[128,64]{1,0:T(8,128)}, f32[8,128]{1,0:T(8,128)}) custom-call(bf16[8,16384]{1,0:T(8,128)(2,1)} %charges_hbm.1, f32[16,16,128]{2,1,0:T(8,128)} %get-tuple-element.12.block_hbm, bf16[9,128,2048]{2,1,0:T(8,128)(2,1)} %get-tuple-element.13.table_hbm, s32[1,512]{1,0:T(1,128)} %get-tuple-element.14.list_hbm), custom_call_target="tpu_custom_call" | custom-call | tf_op jit(solution)/shard_map/local_part/pallas_call | solution.py:455
  18.3 11.6 %reduce_part.1 = (f32[8,8,8,128]{3,2,1,0:T(8,128)}, f32[8,8,128]{2,1,0:T(8,128)}, f32[64,64]{1,0:T(8,128)}) custom-call(f32[8,8,8,128]{3,2,1,0:T(8,128)} %get-tuple-element.15.part_ref, f32[8,128]{1,0:T(8,128)} %get-tuple-element.16.sq_hbm, f32[128,64]{1,0:T(8,128)} %get-tuple-element.17.moments_hbm, bf16[2,16,64,512]{3,2,1,0:T(8,128)(2,1)} %get-tuple-element.18.phi_hbm), custom_call_target="tpu_custom_call" | custom-call | tf_op jit(solution)/shard_map/reduce_part/pallas_call | solution.py:666
  29.9 2.0 %finish.1 = (bf16[8,1024]{1,0:T(8,128)(2,1)}, f32[64,64]{1,0:T(8,128)}) custom-call(f32[8,8,8,128]{3,2,1,0:T(8,128)} %get-tuple-element.19.recv, f32[8,8,128]{2,1,0:T(8,128)} %get-tuple-element.20.far_recv, f32[64,64]{1,0:T(8,128)} %get-tuple-element.21.root, s32[1,1024]{1,0:T(1,128)} %order_ref.1, f32[64,128]{1,0:T(8,128)} %bitcast.2), custom_call_target="tpu_custom_call" | custom-call | tf_op jit(solution)/shard_map/finish/pallas_call | solution.py:719
